TPU v7x, 512 devices: a whole 4x8x8 slice. The times are simulated.
512 devices in a mesh: xy: 128 (over x, y_hi, z, core), gz: 4 (over y_lo).
Axes of the slice: x: 4, y: 8 (y_hi: 2, y_lo: 4; y = y_hi * 4 + y_lo), z: 8, core: 2. Of those that a mesh axis runs over, the one named last changes fastest.
Arguments:
- density: float32 [16384, 2048], P('xy', 'gz'), may hold values from 0 to 1
- cotangent: float32 [6, 16, 2048, 256], P(None, 'gz', 'xy'), may hold values from -6 to 6
- slope: int32 [16], P('gz'), may hold values from 0 to 4
- layer_block: int32 [16], P('gz'), may hold values from 0 to 3
- block_eps: float32 [4, 2], replicated, may hold values from 1.5 to 12
Outputs:
- grad_filtered: float32 [16384, 2048], P('xy', 'gz')
- grad_density: float32 [16384, 2048], P('xy', 'gz')
All inputs are finite; a program needn't handle non-finite values.
Results may differ from a plain program's by a relative error of at most 0.0003.
Values sent between devices are 32-bit elements; how exact they have to be, the bound alone decides.
No kernel may reach another device: no remote copies, remote signals or barrier semaphores. Data moves between devices by JAX's collectives and lax.ppermute only.
A program may use at most 64 MiB of HBM per device.

v0:
```python
import jax
import jax.numpy as jnp
from jax import lax
from jax.sharding import PartitionSpec as P

SUB = 8
RADIUS = 32
MATS = 4


def padded_2(value, sides, width):
    for axis, dim in sides:
        count, length = (lax.axis_size(axis), value.shape[dim])
        up = [(i, (i + 1) % count) for i in range(count - 1)]
        down = [(j, i) for i, j in up]
        last = lax.slice_in_dim(value, length - width, length, axis=dim)
        leading = lax.slice_in_dim(value, 0, width, axis=dim)
        before = lax.ppermute(last, axis, up)
        after = lax.ppermute(leading, axis, down)
        value = jnp.concatenate([before, value, after], axis=dim)
    return value


def from_everyone(value, axis):
    copies = jnp.broadcast_to(value, (lax.axis_size(axis), *value.shape))
    return lax.all_to_all(copies, axis, split_axis=0, concat_axis=0, tiled=True)


def joined_along(pieces, dim):
    pieces = jnp.moveaxis(pieces, 0, dim)
    dims = pieces.shape
    return pieces.reshape(*dims[:dim], dims[dim] * dims[dim + 1], *dims[dim + 2 :])


def collect(value, axis, dim):
    pieces = from_everyone(value, axis)
    return joined_along(pieces, dim)


def in_blocks(value, dim, count):
    before, after = (value.shape[:dim], value.shape[dim + 1 :])
    return jnp.moveaxis(value.reshape(*before, count, -1, *after), dim, 0)


def sum_at_owner(value, axis, dim):
    count = lax.axis_size(axis)
    pieces = lax.all_to_all(in_blocks(value, dim, count), axis, 0, 0, tiled=True)
    return jnp.sum(pieces, axis=0)


def band(width):
    rows = lax.broadcasted_iota(jnp.int32, (width + 2 * RADIUS, width), 0)
    cols = lax.broadcasted_iota(jnp.int32, (width + 2 * RADIUS, width), 1)
    offset = rows - cols
    values = (RADIUS + 1 - jnp.abs(offset - RADIUS)).astype(jnp.float32) / float((RADIUS + 1) ** 2)
    return jnp.where((offset >= 0) & (offset <= 2 * RADIUS), values, 0.0)


def smooth(padded):
    height = padded.shape[0] - 2 * RADIUS
    width = padded.shape[1] - 2 * RADIUS
    step_cols = 256
    matrix = band(step_cols)
    pieces = []
    for index in range(width // step_cols):
        part = padded[:, index * step_cols : index * step_cols + step_cols + 2 * RADIUS]
        pieces.append(jnp.dot(part, matrix, precision=lax.Precision.HIGHEST))
    across = jnp.concatenate(pieces, axis=1)
    return jnp.dot(band(height).T, across, precision=lax.Precision.HIGHEST)


def row_pooling(height):
    cells = height // SUB
    rows = lax.broadcasted_iota(jnp.int32, (2 * cells, height), 0)
    pixel = lax.broadcasted_iota(jnp.int32, (2 * cells, height), 1)
    cell_row = jnp.where(rows < cells, rows, rows - cells)
    inside = pixel // SUB == cell_row
    place = (2.0 * (pixel % SUB).astype(jnp.float32) + 1.0 - SUB) / 2.0
    values = jnp.where(rows < cells, 1.0, place) / float(SUB)
    return jnp.where(inside, values, 0.0)


def col_pooling(width):
    cells = width // SUB
    pixel = lax.broadcasted_iota(jnp.int32, (width, cells), 0)
    cols = lax.broadcasted_iota(jnp.int32, (width, cells), 1)
    inside = pixel // SUB == cols
    place = (2.0 * (pixel % SUB).astype(jnp.float32) + 1.0 - SUB) / 2.0
    mean_cols = jnp.where(inside, 1.0 / float(SUB), 0.0)
    offset_cols = jnp.where(inside, place / float(SUB), 0.0)
    return (mean_cols, offset_cols)


def cell_tensor(field, params):
    eta, lift, eps_one, eps_two = (params[0], params[1], params[2], params[3])
    height, width = field.shape
    cells = height // SUB
    fill = jax.nn.sigmoid(32.0 * (field - eta))
    pooled_rows = jnp.dot(row_pooling(height), fill, precision=lax.Precision.HIGHEST)
    mean_cols, offset_cols = col_pooling(width)
    both = jnp.dot(pooled_rows, mean_cols, precision=lax.Precision.HIGHEST)
    frac = both[:cells]
    grad_x = both[cells:]
    grad_y = jnp.dot(pooled_rows[:cells], offset_cols, precision=lax.Precision.HIGHEST)
    normsq = grad_x * grad_x + grad_y * grad_y + lift * lift
    mean_eps = eps_two + frac * (eps_one - eps_two)
    mean_inv = 1.0 / eps_two + frac * (1.0 / eps_one - 1.0 / eps_two)
    weight = (1.0 / mean_inv - mean_eps) / normsq
    return jnp.stack(
        [
            mean_eps + weight * grad_x * grad_x,
            mean_eps + weight * grad_y * grad_y,
            mean_eps + weight * lift * lift,
            weight * grad_x * grad_y,
            weight * grad_x * lift,
            weight * grad_y * lift,
        ]
    )


def pull_layers(field, cotangent, table):

    def step(index, total):
        params = lax.dynamic_index_in_dim(table, index, 1, keepdims=False)
        weights = lax.dynamic_index_in_dim(cotangent, index, 1, keepdims=False)
        pullback = jax.vjp(lambda inner: cell_tensor(inner, params), field)[1]
        return total + pullback(weights)[0]

    return lax.fori_loop(0, cotangent.shape[1], step, jnp.zeros_like(field))


def forward_piece(density):
    padded = padded_2(density, (("xy", 0), ("gz", 1)), RADIUS)
    return smooth(padded)


def backward_piece(own):
    padded = padded_2(own, (("xy", 0), ("gz", 1)), RADIUS)
    return smooth(padded)


def on_device(density, cotangent, slope, layer_block, block_eps):
    level = slope.astype(jnp.float32)
    onehot = (layer_block[:, None] == jnp.arange(MATS)[None, :]).astype(jnp.float32)
    pairs = jnp.dot(onehot, block_eps, precision=lax.Precision.HIGHEST)
    table = jnp.stack([0.5 + 0.02 * (level - 2.0), 0.2 * (1.0 + level), pairs[:, 0], pairs[:, 1]])
    filtered = collect(forward_piece(density), "gz", 1)
    partial_grad = pull_layers(filtered, cotangent, table)
    own = sum_at_owner(partial_grad, "gz", 1)
    result = backward_piece(own)
    return (own, result)


def solution(mesh):
    return jax.shard_map(
        on_device,
        mesh=mesh,
        in_specs=(P("xy", "gz"), P(None, "gz", "xy", None), P("gz"), P("gz"), P()),
        out_specs=(P("xy", "gz"), P("xy", "gz")),
        check_vma=False,
    )
```

profile of v0, /device:TPU:6, one launch (start us, length us, event | category | flops | bytes accessed | tf_op | source)
XLA Modules:
  0.0 195.5 jit_solution(14642178630299371747)
XLA Ops:
  3.5 15.9 %collective-permute-start.1 = (f32[32,512]{1,0:T(8,128)S(1)}, f32[32,512]{1,0:T(8,128)S(1)}, u32[]{:S(2)}, u32[]{:S(2)}) collective-permute-start(f32[32,512]{1,0:T(8,128)S(1)} %get-tuple-element.272), channel_id=1, source_target_pairs={{4,0},{8,4},{12,8},{16,12},{20,16},{24,20},{28,24},{32,28},{36,32}... | collective-permute-start | bytes 196616 | tf_op jit(solution)/shard_map/ppermute | solution.py:19
  26.7 4.1 %collective-permute-done.3 = f32[192,32]{1,0:T(8,128)S(1)} collective-permute-done((f32[192,32]{1,0:T(8,128)S(1)}, f32[192,32]{1,0:T(8,128)S(1)}, u32[]{:S(2)}, u32[]{:S(2)}) %collective-permute-start.3) | collective-permute-done | bytes 24608 | tf_op jit(solution)/shard_map/ppermute | solution.py:19
  32.9 3.6 %all-to-all-start = ((f32[4,128,512]{2,1,0:T(8,128)}), f32[4,128,512]{2,1,0:T(8,128)S(1)}, u32[]{:S(2)}, u32[]{:S(2)}) async-start(f32[4,128,512]{2,1,0:T(8,128)} %broadcast_in_dim.83), calls=%async_computation | async-start | bytes 2097152 | tf_op jit(solution)/shard_map/all_to_all | solution.py:26
  36.8 16.7 %all-to-all-done = f32[4,128,512]{2,1,0:T(8,128)S(1)} async-done(((f32[4,128,512]{2,1,0:T(8,128)}), f32[4,128,512]{2,1,0:T(8,128)S(1)}, u32[]{:S(2)}, u32[]{:S(2)}) %all-to-all-start) | async-done | bytes 1048608 | tf_op jit(solution)/shard_map/all_to_all | solution.py:26
  54.9 84.1 %while.19 = (s32[]{:T(128)}, f32[128,2048]{1,0:T(8,128)S(1)}, f32[4,4]{1,0:T(4,128)S(1)}, f32[128,2048]{1,0:T(8,128)S(1)}, f32[6,4,16,256]{3,2,1,0:T(8,128)S(1)}...) while((s32[]{:T(128)}, f32[128,2048]{1,0:T(8,128)S(1)}, ...), condition=%wide.region_1.2_spmd.clone, body=%wide.region_0.1_spmd.clone.sunk | while | flops 821595840 | bytes 6284447 | solution.py:129
  62.9 3.7 %add_add_fusion.8 = (f32[16,256]{1,0:T(8,128)S(1)}, f32[16,256]{1,0:T(8,128)S(1)}, f32[16,256]{1,0:T(8,128)S(1)}) fusion(f32[6,4,16,256]{3,2,1,0:T(8,128)S(1)} %get-tuple-element.377, s32[]{:T(128)S(6)} %add.440, s32[]{:T(128)S(6)} %copy.15, s32[]{:T(128)S(6)} %add.441, f32[32,256]{1,0:T(8,128)S(1)} %fusion.247, f32[]{:T(128)} %bitcast.101, ...), kind=kOutput, calls=%fused_computation.49.clone.1 | convolution fusion | flops 105033728 | bytes 349736 | tf_op jit(solution)/shard_map/while/body/eval_jaxpr/jvp()/dot_general | solution.py:104
  66.7 4.5 %fusion.248 = f32[16,2048]{1,0:T(8,128)S(1)} fusion(s32[2048]{0:T(1024)S(1)} %get-tuple-element.331, s32[2048]{0:T(1024)S(1)} %get-tuple-element.332, s32[2048]{0:T(1024)S(1)} %get-tuple-element.328, s32[2048]{0:T(1024)S(1)} %get-tuple-element.329, pred[2048]{0:T(1024)(128)(4,1)S(1)} %get-tuple-element.333, ...), kind=kOutput, calls=%fused_computation.9.clone.1 | convolution fusion | flops 104980480 | bytes 282664 | tf_op jit(solution)/shard_map/while/body/eval_jaxpr/transpose(jvp())/dot_general | solution.py:104
  71.1 2.4 %fusion.249 = f32[32,2048]{1,0:T(8,128)S(1)} fusion(s32[2048]{0:T(1024)S(1)} %get-tuple-element.328, s32[2048]{0:T(1024)S(1)} %get-tuple-element.329, pred[2048]{0:T(1024)(128)(4,1)S(1)} %get-tuple-element.330, f32[16,2048]{1,0:T(8,128)S(1)} %fusion.248, f32[16,256]{1,0:T(8,128)S(1)} %multiply_add_fusion.6, f32[16,256]{1,0:T(8,128)S(1)} %get-tuple-element.346), kind=kOutput, calls=%fused_computation.7.clone.1 | convolution fusion | flops 202973184 | bytes 444416 | tf_op jit(solution)/shard_map/while/body/eval_jaxpr/transpose(jvp())/dot_general | solution.py:101
  73.6 2.3 %fusion.250 = f32[128,2048]{1,0:T(8,128)S(1)} fusion(f32[32,2048]{1,0:T(8,128)S(1)} %fusion.249, f32[128,2048]{1,0:T(8,128)S(1)} %get-tuple-element.361, pred[]{:T(512)S(6)} %compare.14, f32[128,2048]{1,0:T(8,128)S(1)} %get-tuple-element.376, f32[]{:T(128)} %bitcast.100, s32[128]{0:T(128)S(1)} %get-tuple-element.335, s32[128]{0:T(128)S(1)} %get-tuple-element.336, ...), kind=kOutput, calls=%fused_computation.6.clone.1 | convolution fusion | flops 103591936 | bytes 3410341 | tf_op jit(solution)/shard_map/while/body/eval_jaxpr/transpose(jvp())/dot_general | solution.py:99
  84.0 3.7 %add_add_fusion.8 = (f32[16,256]{1,0:T(8,128)S(1)}, f32[16,256]{1,0:T(8,128)S(1)}, f32[16,256]{1,0:T(8,128)S(1)}) fusion(f32[6,4,16,256]{3,2,1,0:T(8,128)S(1)} %get-tuple-element.377, s32[]{:T(128)S(6)} %add.440, s32[]{:T(128)S(6)} %copy.15, s32[]{:T(128)S(6)} %add.441, f32[32,256]{1,0:T(8,128)S(1)} %fusion.247, f32[]{:T(128)} %bitcast.101, ...), kind=kOutput, calls=%fused_computation.49.clone.1 | convolution fusion | flops 105033728 | bytes 349736 | tf_op jit(solution)/shard_map/while/body/eval_jaxpr/jvp()/dot_general | solution.py:104
  87.7 4.5 %fusion.248 = f32[16,2048]{1,0:T(8,128)S(1)} fusion(s32[2048]{0:T(1024)S(1)} %get-tuple-element.331, s32[2048]{0:T(1024)S(1)} %get-tuple-element.332, s32[2048]{0:T(1024)S(1)} %get-tuple-element.328, s32[2048]{0:T(1024)S(1)} %get-tuple-element.329, pred[2048]{0:T(1024)(128)(4,1)S(1)} %get-tuple-element.333, ...), kind=kOutput, calls=%fused_computation.9.clone.1 | convolution fusion | flops 104980480 | bytes 282664 | tf_op jit(solution)/shard_map/while/body/eval_jaxpr/transpose(jvp())/dot_general | solution.py:104
  92.2 2.4 %fusion.249 = f32[32,2048]{1,0:T(8,128)S(1)} fusion(s32[2048]{0:T(1024)S(1)} %get-tuple-element.328, s32[2048]{0:T(1024)S(1)} %get-tuple-element.329, pred[2048]{0:T(1024)(128)(4,1)S(1)} %get-tuple-element.330, f32[16,2048]{1,0:T(8,128)S(1)} %fusion.248, f32[16,256]{1,0:T(8,128)S(1)} %multiply_add_fusion.6, f32[16,256]{1,0:T(8,128)S(1)} %get-tuple-element.346), kind=kOutput, calls=%fused_computation.7.clone.1 | convolution fusion | flops 202973184 | bytes 444416 | tf_op jit(solution)/shard_map/while/body/eval_jaxpr/transpose(jvp())/dot_general | solution.py:101
  94.6 2.3 %fusion.250 = f32[128,2048]{1,0:T(8,128)S(1)} fusion(f32[32,2048]{1,0:T(8,128)S(1)} %fusion.249, f32[128,2048]{1,0:T(8,128)S(1)} %get-tuple-element.361, pred[]{:T(512)S(6)} %compare.14, f32[128,2048]{1,0:T(8,128)S(1)} %get-tuple-element.376, f32[]{:T(128)} %bitcast.100, s32[128]{0:T(128)S(1)} %get-tuple-element.335, s32[128]{0:T(128)S(1)} %get-tuple-element.336, ...), kind=kOutput, calls=%fused_computation.6.clone.1 | convolution fusion | flops 103591936 | bytes 3410341 | tf_op jit(solution)/shard_map/while/body/eval_jaxpr/transpose(jvp())/dot_general | solution.py:99
  105.0 3.7 %add_add_fusion.8 = (f32[16,256]{1,0:T(8,128)S(1)}, f32[16,256]{1,0:T(8,128)S(1)}, f32[16,256]{1,0:T(8,128)S(1)}) fusion(f32[6,4,16,256]{3,2,1,0:T(8,128)S(1)} %get-tuple-element.377, s32[]{:T(128)S(6)} %add.440, s32[]{:T(128)S(6)} %copy.15, s32[]{:T(128)S(6)} %add.441, f32[32,256]{1,0:T(8,128)S(1)} %fusion.247, f32[]{:T(128)} %bitcast.101, ...), kind=kOutput, calls=%fused_computation.49.clone.1 | convolution fusion | flops 105033728 | bytes 349736 | tf_op jit(solution)/shard_map/while/body/eval_jaxpr/jvp()/dot_general | solution.py:104
  108.7 4.5 %fusion.248 = f32[16,2048]{1,0:T(8,128)S(1)} fusion(s32[2048]{0:T(1024)S(1)} %get-tuple-element.331, s32[2048]{0:T(1024)S(1)} %get-tuple-element.332, s32[2048]{0:T(1024)S(1)} %get-tuple-element.328, s32[2048]{0:T(1024)S(1)} %get-tuple-element.329, pred[2048]{0:T(1024)(128)(4,1)S(1)} %get-tuple-element.333, ...), kind=kOutput, calls=%fused_computation.9.clone.1 | convolution fusion | flops 104980480 | bytes 282664 | tf_op jit(solution)/shard_map/while/body/eval_jaxpr/transpose(jvp())/dot_general | solution.py:104
  113.2 2.4 %fusion.249 = f32[32,2048]{1,0:T(8,128)S(1)} fusion(s32[2048]{0:T(1024)S(1)} %get-tuple-element.328, s32[2048]{0:T(1024)S(1)} %get-tuple-element.329, pred[2048]{0:T(1024)(128)(4,1)S(1)} %get-tuple-element.330, f32[16,2048]{1,0:T(8,128)S(1)} %fusion.248, f32[16,256]{1,0:T(8,128)S(1)} %multiply_add_fusion.6, f32[16,256]{1,0:T(8,128)S(1)} %get-tuple-element.346), kind=kOutput, calls=%fused_computation.7.clone.1 | convolution fusion | flops 202973184 | bytes 444416 | tf_op jit(solution)/shard_map/while/body/eval_jaxpr/transpose(jvp())/dot_general | solution.py:101
  115.7 2.3 %fusion.250 = f32[128,2048]{1,0:T(8,128)S(1)} fusion(f32[32,2048]{1,0:T(8,128)S(1)} %fusion.249, f32[128,2048]{1,0:T(8,128)S(1)} %get-tuple-element.361, pred[]{:T(512)S(6)} %compare.14, f32[128,2048]{1,0:T(8,128)S(1)} %get-tuple-element.376, f32[]{:T(128)} %bitcast.100, s32[128]{0:T(128)S(1)} %get-tuple-element.335, s32[128]{0:T(128)S(1)} %get-tuple-element.336, ...), kind=kOutput, calls=%fused_computation.6.clone.1 | convolution fusion | flops 103591936 | bytes 3410341 | tf_op jit(solution)/shard_map/while/body/eval_jaxpr/transpose(jvp())/dot_general | solution.py:99
  126.1 3.7 %add_add_fusion.8 = (f32[16,256]{1,0:T(8,128)S(1)}, f32[16,256]{1,0:T(8,128)S(1)}, f32[16,256]{1,0:T(8,128)S(1)}) fusion(f32[6,4,16,256]{3,2,1,0:T(8,128)S(1)} %get-tuple-element.377, s32[]{:T(128)S(6)} %add.440, s32[]{:T(128)S(6)} %copy.15, s32[]{:T(128)S(6)} %add.441, f32[32,256]{1,0:T(8,128)S(1)} %fusion.247, f32[]{:T(128)} %bitcast.101, ...), kind=kOutput, calls=%fused_computation.49.clone.1 | convolution fusion | flops 105033728 | bytes 349736 | tf_op jit(solution)/shard_map/while/body/eval_jaxpr/jvp()/dot_general | solution.py:104
  129.8 4.5 %fusion.248 = f32[16,2048]{1,0:T(8,128)S(1)} fusion(s32[2048]{0:T(1024)S(1)} %get-tuple-element.331, s32[2048]{0:T(1024)S(1)} %get-tuple-element.332, s32[2048]{0:T(1024)S(1)} %get-tuple-element.328, s32[2048]{0:T(1024)S(1)} %get-tuple-element.329, pred[2048]{0:T(1024)(128)(4,1)S(1)} %get-tuple-element.333, ...), kind=kOutput, calls=%fused_computation.9.clone.1 | convolution fusion | flops 104980480 | bytes 282664 | tf_op jit(solution)/shard_map/while/body/eval_jaxpr/transpose(jvp())/dot_general | solution.py:104
  134.3 2.4 %fusion.249 = f32[32,2048]{1,0:T(8,128)S(1)} fusion(s32[2048]{0:T(1024)S(1)} %get-tuple-element.328, s32[2048]{0:T(1024)S(1)} %get-tuple-element.329, pred[2048]{0:T(1024)(128)(4,1)S(1)} %get-tuple-element.330, f32[16,2048]{1,0:T(8,128)S(1)} %fusion.248, f32[16,256]{1,0:T(8,128)S(1)} %multiply_add_fusion.6, f32[16,256]{1,0:T(8,128)S(1)} %get-tuple-element.346), kind=kOutput, calls=%fused_computation.7.clone.1 | convolution fusion | flops 202973184 | bytes 444416 | tf_op jit(solution)/shard_map/while/body/eval_jaxpr/transpose(jvp())/dot_general | solution.py:101
  136.7 2.3 %fusion.250 = f32[128,2048]{1,0:T(8,128)S(1)} fusion(f32[32,2048]{1,0:T(8,128)S(1)} %fusion.249, f32[128,2048]{1,0:T(8,128)S(1)} %get-tuple-element.361, pred[]{:T(512)S(6)} %compare.14, f32[128,2048]{1,0:T(8,128)S(1)} %get-tuple-element.376, f32[]{:T(128)} %bitcast.100, s32[128]{0:T(128)S(1)} %get-tuple-element.335, s32[128]{0:T(128)S(1)} %get-tuple-element.336, ...), kind=kOutput, calls=%fused_computation.6.clone.1 | convolution fusion | flops 103591936 | bytes 3410341 | tf_op jit(solution)/shard_map/while/body/eval_jaxpr/transpose(jvp())/dot_general | solution.py:99
  139.7 21.1 %all_to_all.10 = f32[4,128,512]{2,1,0:T(8,128)S(1)} all-to-all(f32[4,128,512]{2,1,0:T(8,128)S(1)} %copy.10), channel_id=1, replica_groups=mesh['xy'=128,'gz'=4] {'gz'}, dimensions={0} | all-to-all | bytes 2097152 | tf_op jit(solution)/shard_map/all_to_all | solution.py:47
  162.8 20.3 %collective-permute-start.5 = (f32[32,512]{1,0:T(8,128)S(1)}, f32[32,512]{1,0:T(8,128)S(1)}, u32[]{:S(2)}, u32[]{:S(2)}) collective-permute-start(f32[32,512]{1,0:T(8,128)S(1)} %get-tuple-element.271), channel_id=1, source_target_pairs={{4,0},{8,4},{12,8},{16,12},{20,16},{24,20},{28,24},{32,28},{36,32}... | collective-permute-start | bytes 196616 | tf_op jit(solution)/shard_map/ppermute | solution.py:19
  190.0 3.8 %collective-permute-done.7 = f32[192,32]{1,0:T(8,128)S(1)} collective-permute-done((f32[192,32]{1,0:T(8,128)S(1)}, f32[192,32]{1,0:T(8,128)S(1)}, u32[]{:S(2)}, u32[]{:S(2)}) %collective-permute-start.7) | collective-permute-done | bytes 24608 | tf_op jit(solution)/shard_map/ppermute | solution.py:19
  (98 shorter events, 40.7 us)
Async XLA Ops:
  0.6 36.0 %copy-start = (f32[4,2]{0,1:T(2,128)S(1)}, f32[4,2]{0,1:T(2,128)}, u32[]{:S(2)}) copy-start(f32[4,2]{0,1:T(2,128)} %param.11) | copy-start | bytes 100
  1.5 18.5 %collective-permute-start = (f32[32,512]{1,0:T(8,128)S(1)}, f32[32,512]{1,0:T(8,128)S(1)}, u32[]{:S(2)}, u32[]{:S(2)}) collective-permute-start(f32[32,512]{1,0:T(8,128)S(1)} %get-tuple-element.273), channel_id=1, source_target_pairs={{0,4},{4,8},{8,12},{12,16},{16,20},{20,24},{24,28},{28,32},{32,36}... | collective-permute-start | bytes 196616 | tf_op jit(solution)/shard_map/ppermute | solution.py:18
  3.5 18.2 %collective-permute-start.1 = (f32[32,512]{1,0:T(8,128)S(1)}, f32[32,512]{1,0:T(8,128)S(1)}, u32[]{:S(2)}, u32[]{:S(2)}) collective-permute-start(f32[32,512]{1,0:T(8,128)S(1)} %get-tuple-element.272), channel_id=1, source_target_pairs={{4,0},{8,4},{12,8},{16,12},{20,16},{24,20},{28,24},{32,28},{36,32}... | collective-permute-start | bytes 196616 | tf_op jit(solution)/shard_map/ppermute | solution.py:19
  21.8 4.4 %collective-permute-start.2 = (f32[192,32]{1,0:T(8,128)S(1)}, f32[192,32]{1,0:T(8,128)S(1)}, u32[]{:S(2)}, u32[]{:S(2)}) collective-permute-start(f32[192,32]{1,0:T(8,128)S(1)} %get-tuple-element.268), channel_id=1, source_target_pairs={{0,1},{1,2},{2,3},{4,5},{5,6},{6,7},{8,9},{9,10},{10,11},{12,13},{... | collective-permute-start | bytes 73736 | tf_op jit(solution)/shard_map/ppermute | solution.py:18
  24.0 6.8 %collective-permute-start.3 = (f32[192,32]{1,0:T(8,128)S(1)}, f32[192,32]{1,0:T(8,128)S(1)}, u32[]{:S(2)}, u32[]{:S(2)}) collective-permute-start(f32[192,32]{1,0:T(8,128)S(1)} %get-tuple-element.269), channel_id=1, source_target_pairs={{1,0},{2,1},{3,2},{5,4},{6,5},{7,6},{9,8},{10,9},{11,10},{13,12},{... | collective-permute-start | bytes 73736 | tf_op jit(solution)/shard_map/ppermute | solution.py:19
  32.9 3.7 %copy-start.3 = (s32[4]{0:T(128)S(1)}, s32[4]{0:T(128)}, u32[]{:S(2)}) copy-start(s32[4]{0:T(128)} %param.9) | copy-start | bytes 52
  32.9 3.7 %copy-start.4 = (s32[4]{0:T(128)S(1)}, s32[4]{0:T(128)}, u32[]{:S(2)}) copy-start(s32[4]{0:T(128)} %param.10) | copy-start | bytes 52
  32.9 20.6 %all-to-all-start = ((f32[4,128,512]{2,1,0:T(8,128)}), f32[4,128,512]{2,1,0:T(8,128)S(1)}, u32[]{:S(2)}, u32[]{:S(2)}) async-start(f32[4,128,512]{2,1,0:T(8,128)} %broadcast_in_dim.83), calls=%async_computation | async-start | bytes 2097152 | tf_op jit(solution)/shard_map/all_to_all | solution.py:26
  53.9 1.0 copy-start.2
  160.9 32.9 %copy-start.1 = (f32[128,512]{1,0:T(8,128)}, f32[128,512]{1,0:T(8,128)S(1)}, u32[]{:S(2)}) copy-start(f32[128,512]{1,0:T(8,128)S(1)} %reduce_sum.9) | copy-start | bytes 786436
  160.9 22.3 %collective-permute-start.4 = (f32[32,512]{1,0:T(8,128)S(1)}, f32[32,512]{1,0:T(8,128)S(1)}, u32[]{:S(2)}, u32[]{:S(2)}) collective-permute-start(f32[32,512]{1,0:T(8,128)S(1)} %get-tuple-element.270), channel_id=1, source_target_pairs={{0,4},{4,8},{8,12},{12,16},{16,20},{20,24},{24,28},{28,32},{32,36}... | collective-permute-start | bytes 196616 | tf_op jit(solution)/shard_map/ppermute | solution.py:18
  162.8 22.2 %collective-permute-start.5 = (f32[32,512]{1,0:T(8,128)S(1)}, f32[32,512]{1,0:T(8,128)S(1)}, u32[]{:S(2)}, u32[]{:S(2)}) collective-permute-start(f32[32,512]{1,0:T(8,128)S(1)} %get-tuple-element.271), channel_id=1, source_target_pairs={{4,0},{8,4},{12,8},{16,12},{20,16},{24,20},{28,24},{32,28},{36,32}... | collective-permute-start | bytes 196616 | tf_op jit(solution)/shard_map/ppermute | solution.py:19
  185.1 4.3 %collective-permute-start.6 = (f32[192,32]{1,0:T(8,128)S(1)}, f32[192,32]{1,0:T(8,128)S(1)}, u32[]{:S(2)}, u32[]{:S(2)}) collective-permute-start(f32[192,32]{1,0:T(8,128)S(1)} %get-tuple-element.266), channel_id=1, source_target_pairs={{0,1},{1,2},{2,3},{4,5},{5,6},{6,7},{8,9},{9,10},{10,11},{12,13},{... | collective-permute-start | bytes 73736 | tf_op jit(solution)/shard_map/ppermute | solution.py:18
  187.3 6.5 %collective-permute-start.7 = (f32[192,32]{1,0:T(8,128)S(1)}, f32[192,32]{1,0:T(8,128)S(1)}, u32[]{:S(2)}, u32[]{:S(2)}) collective-permute-start(f32[192,32]{1,0:T(8,128)S(1)} %get-tuple-element.267), channel_id=1, source_target_pairs={{1,0},{2,1},{3,2},{5,4},{6,5},{7,6},{9,8},{10,9},{11,10},{13,12},{... | collective-permute-start | bytes 73736 | tf_op jit(solution)/shard_map/ppermute | solution.py:19
where the time goes:
time: 196 us
  matrix products  68.3 us (35%)
  starting transfers between devices  50.6 us (26%)
  waiting for transfers between devices  29.5 us (15%)
  blocking collectives  21.1 us (11%)
  loops' own time  16.9 us (9%)
  local copies, waits for them, and re-layouts  7.84 us (4%)
    ppermute x4, starting transfers between devices, padded_2(): after = lax.ppermute(leading, axis, down)  38.8 us
    dot_general x8, matrix products, cell_tensor(): jnp.dot(pooled_rows[:cells], offset_cols, precision=lax.Precision.HIGHEST)  32.6 us
    all_to_all x1, blocking collectives, sum_at_owner(): lax.all_to_all(in_blocks(value, dim, count), axis, 0, 0, tiled=True)  21.1 us
    another operation x1, loops' own time, pull_layers(): return lax.fori_loop(0, cotangent.shape[1], step, jnp.zeros_like(field))  16.9 us
    all_to_all x1, waiting for transfers between devices, from_everyone(): return lax.all_to_all(copies, axis, split_axis=0, concat_axis=0, tiled=True)  16.7 us
    dot_general x8, matrix products, cell_tensor(): both = jnp.dot(pooled_rows, mean_cols, precision=lax.Precision.HIGHEST)  16.5 us
    dot_general x8, matrix products, cell_tensor(): jnp.dot(row_pooling(height), fill, precision=lax.Precision.HIGHEST)  15.2 us
    ppermute x4, waiting for transfers between devices, padded_2(): after = lax.ppermute(leading, axis, down)  10.3 us
  transfers between devices with their start and end apart: 9, of which 8 were waited for; matrix products, arithmetic and copies ran while one was open for 1% of the time, Pallas kernels for 0%

commit v1 on v0

v1 whole, which is shorter than its diff:
```python
import functools
import math

import jax
import jax.numpy as jnp
from jax import lax
from jax.experimental import pallas as pl
from jax.experimental.pallas import tpu as pltpu
from jax.sharding import PartitionSpec as P

SUB = 8
RADIUS = 32
MATS = 4
SLOPES = 5
SCALE = 1.0 / float((RADIUS + 1) ** 2)
BF = jnp.bfloat16
F32 = jnp.float32
VMEM = pl.BlockSpec(memory_space=pltpu.VMEM)
SMEM = pl.BlockSpec(memory_space=pltpu.SMEM)
LIMIT = 24 << 20

HEIGHT = 128
WIDTH = 512
WIDE = WIDTH + 2 * RADIUS
CELLS = WIDE // SUB
ROWS = 224


def iota(shape, dim):
    return lax.broadcasted_iota(jnp.int32, shape, dim)


def parts_of(value, count):
    parts = []
    for index in range(count):
        part = value.astype(BF)
        parts.append(part)
        if index + 1 < count:
            value = value - part.astype(F32)
    return parts


def band(rows, cols):
    offset = iota((rows, cols), 1) - iota((rows, cols), 0) - RADIUS
    return jnp.maximum(RADIUS + 1 - jnp.abs(offset), 0).astype(F32).astype(BF)


def dot(a, b):
    return jnp.dot(a, b, preferred_element_type=F32)


def place_lanes():
    return (iota((1, HEIGHT), 1) % SUB).astype(F32) - 3.5


def call(body, name, outs, scratch, flops, moved, *args, smem=()):
    return pl.pallas_call(
        body,
        name=name,
        out_shape=[jax.ShapeDtypeStruct(shape, F32) for shape in outs],
        in_specs=[SMEM if index in smem else VMEM for index in range(len(args))],
        out_specs=[VMEM for _ in outs],
        scratch_shapes=[pltpu.VMEM(shape, F32) for shape in scratch],
        compiler_params=pltpu.CompilerParams(vmem_limit_bytes=LIMIT),
        cost_estimate=pl.CostEstimate(flops=flops, bytes_accessed=moved, transcendentals=0),
    )(*args)


def pack_body(slope, block, eps, cot, send):
    low = iota((SUB, HEIGHT), 0) < 4
    zero = jnp.zeros((SUB, HEIGHT), F32)
    for slab in range(3):
        turned = cot[slab * 128 : slab * 128 + 128, :].T
        for owner in range(4):
            first, base = (64 * owner, 72 * slab)
            send[owner, base : base + 64, :] = turned[first : first + 64]
            after = zero if owner == 3 else turned[first + 64 : first + 72]
            before = zero if owner == 0 else turned[first - 8 : first]
            send[owner, base + 64 : base + 72, :] = jnp.where(low, after, before)
    layer = (iota((SUB, HEIGHT), 1) % 64) // 16
    row = iota((SUB, HEIGHT), 0)
    table = zero
    for index in range(4):
        one = eps[block[index], 0]
        two = eps[block[index], 1]
        level = slope[index].astype(F32)
        column = jnp.where(row == 0, level, jnp.where(row == 1, one, jnp.where(row == 2, two, 0.0)))
        table = jnp.where(layer == index, column, table)
    for owner in range(4):
        send[owner, 216:224, :] = table


def rows_body(top, own, bottom, out, first, last):
    padded = jnp.concatenate([top[...], own[...], bottom[...]], axis=0)
    matrix = band(HEIGHT, HEIGHT + 2 * RADIUS)
    total = None
    for part in parts_of(padded, 3):
        term = dot(matrix, part)
        total = term if total is None else total + term
    turned = (total * SCALE).T
    out[...] = turned
    first[...] = turned[:64]
    last[...] = turned[WIDTH - 64 :]


def forward_body(left, own, right, expo, pooled, natural):
    padded = jnp.concatenate([left[...], own[...], right[...]], axis=0)
    padded = jnp.concatenate(parts_of(padded, 3), axis=1)
    matrix = band(192, 256)
    for block in range(3):
        wide = dot(matrix, padded[192 * block : 192 * block + 256])
        field = (wide[:, :128] + wide[:, 128:256] + wide[:, 256:]) * SCALE
        value = jnp.exp(16.0 - 32.0 * field)
        if block == 0:
            natural[WIDTH + RADIUS : WIDE, :] = value[:RADIUS]
            natural[: 192 - RADIUS, :] = value[RADIUS:]
        else:
            natural[192 * block - RADIUS : 192 * block - RADIUS + 192, :] = value
    for q in range(SUB):
        expo[q] = natural[pl.ds(q, CELLS, stride=SUB), :]
    place = place_lanes()
    stacks = []
    for s in range(SLOPES):
        factor = math.exp(0.64 * (s - 2))
        mean = jnp.zeros((CELLS, HEIGHT), F32)
        slant = jnp.zeros((CELLS, HEIGHT), F32)
        for q in range(SUB):
            fill = 1.0 / (1.0 + factor * expo[q])
            mean = mean + fill
            slant = slant + (q - 3.5) * fill
        stacks += [mean, mean * place, slant]
    stacks.append(jnp.zeros((SUB, HEIGHT), F32))
    rows = jnp.concatenate(parts_of(jnp.concatenate(stacks, axis=0), 2), axis=1)
    base = ((iota((256, 256), 0) % 128) // SUB == iota((256, 256), 1) % 16).astype(F32).astype(BF)
    pooled[...] = dot(rows, base) * (1.0 / 64.0)


def backward_body(expo, pooled, got, out, turned, top, bottom, natural):
    half = iota((1, 128), 1) < 64
    def pair(a, b):
        return jnp.where(half, a, b)

    def line(row):
        value = [got[g, row : row + 1, :] for g in range(4)]
        return jnp.concatenate([pair(value[0], value[1]), pair(value[2], value[3])], axis=1)

    level, eps_one, eps_two = (line(216), line(217), line(218))
    comps = []
    for slab in range(3):
        value = [got[g, 72 * slab : 72 * slab + 72, :] for g in range(4)]
        swapped = [pltpu.roll(v, 64, 1) for v in value]
        comps.append(jnp.concatenate([pair(value[0], swapped[1]), pair(value[2], swapped[3])], axis=1))
        comps.append(jnp.concatenate([pair(swapped[0], value[1]), pair(swapped[2], value[3])], axis=1))
    cxx, cyy, czz, cxy, cxz, cyz = comps
    frac = jnp.zeros((CELLS, 256), F32)
    grad_x = jnp.zeros((CELLS, 256), F32)
    grad_y = jnp.zeros((CELLS, 256), F32)
    masks = []
    for s in range(SLOPES):
        mask = level == float(s)
        masks.append(mask)
        frac = jnp.where(mask, pooled[216 * s : 216 * s + 72, :], frac)
        grad_x = jnp.where(mask, pooled[216 * s + 72 : 216 * s + 144, :], grad_x)
        grad_y = jnp.where(mask, pooled[216 * s + 144 : 216 * s + 216, :], grad_y)
    lift = 0.2 * (1.0 + level)
    slope_mean = eps_one - eps_two
    inv_two = 1.0 / eps_two
    slope_inv = 1.0 / eps_one - inv_two
    mean_eps = eps_two + frac * slope_mean
    harmonic = 1.0 / (inv_two + frac * slope_inv)
    inv_norm = 1.0 / (grad_x * grad_x + grad_y * grad_y + lift * lift)
    weight = (harmonic - mean_eps) * inv_norm
    along_x = cxx * grad_x + cxy * grad_y + cxz * lift
    along_y = cyy * grad_y + cyz * lift
    quad = grad_x * along_x + grad_y * along_y + czz * (lift * lift)
    trace = cxx + cyy + czz
    d_frac = trace * slope_mean - quad * inv_norm * (harmonic * harmonic * slope_inv + slope_mean)
    shared = 2.0 * inv_norm * quad
    d_x = weight * (along_x + cxx * grad_x - grad_x * shared)
    d_y = weight * (along_y + cyy * grad_y + cxy * grad_x - grad_y * shared)
    stack = jnp.concatenate([d_frac, d_x, d_y, jnp.zeros((SUB, 256), F32)], axis=0) * 0.5
    high, low = parts_of(stack, 2)
    spread = (iota((256, HEIGHT), 0) % 16 == iota((256, HEIGHT), 1) // SUB).astype(F32).astype(BF)
    place = place_lanes()
    flat, tilt = ([], [])
    for mask in masks:
        keep = jnp.where(mask, 1.0, 0.0).astype(BF)
        both = dot(high * keep, spread) + dot(low * keep, spread)
        flat.append(both[:72] + place * both[72:144])
        tilt.append(both[144:216])
    for q in range(SUB):
        total = jnp.zeros((CELLS, HEIGHT), F32)
        for s in range(SLOPES):
            scaled = math.exp(0.64 * (s - 2)) * expo[q]
            fill = 1.0 / (1.0 + scaled)
            total = total + (fill * fill * scaled) * (flat[s] + (q - 3.5) * tilt[s])
        natural[pl.ds(q, CELLS, stride=SUB), :] = total
    out[...] = natural[:WIDTH, :].T
    matrix = band(192, 256)
    pieces = []
    for block in range(3):
        count = 192 if block < 2 else 128
        if block == 0:
            window = jnp.concatenate([natural[WIDTH + RADIUS : WIDE, :], natural[:224, :]], axis=0)
        else:
            window = natural[192 * block - RADIUS : 192 * block + count + RADIUS, :]
        wide = dot(matrix[:count, : count + 64], jnp.concatenate(parts_of(window, 2), axis=1))
        pieces.append((wide[:, :128] + wide[:, 128:]) * SCALE)
    result = jnp.concatenate(pieces, axis=0).T
    turned[...] = result
    top[...] = result[:RADIUS]
    bottom[...] = result[HEIGHT - RADIUS :]


def last_body(top, own, bottom, out):
    padded = jnp.concatenate([top[...], own[...], bottom[...]], axis=0)
    matrix = band(HEIGHT, HEIGHT + 2 * RADIUS)
    high, low = parts_of(padded, 2)
    out[...] = (dot(matrix, high) + dot(matrix, low)) * SCALE


def exchange(leading, trailing, axis):
    count = lax.axis_size(axis)
    up = [(i, i + 1) for i in range(count - 1)]
    down = [(j, i) for i, j in up]
    return (lax.ppermute(trailing, axis, up), lax.ppermute(leading, axis, down))


def on_device(density, cotangent, slope, layer_block, block_eps):
    flat = cotangent.reshape(384, 256)
    (send,) = call(pack_body, "pack", [(4, ROWS, 128)], [], 10**6, 10**6, slope, layer_block, block_eps, flat, smem=(0, 1, 2))
    got = lax.all_to_all(send, "gz", 0, 0, tiled=True)
    before, after = exchange(density[:RADIUS], density[HEIGHT - RADIUS :], "xy")
    across, first, last = call(rows_body, "rows", [(WIDTH, HEIGHT), (64, HEIGHT), (64, HEIGHT)], [], 10**8, 10**6, before, density, after)
    left, right = exchange(first, last, "gz")
    expo, pooled = call(forward_body, "forward", [(SUB, CELLS, HEIGHT), (1088, 256)], [(WIDE, HEIGHT)], 10**8, 2 * 10**6, left, across, right)
    own, turned, top, bottom = call(
        backward_body, "backward", [(HEIGHT, WIDTH), (HEIGHT, WIDTH), (RADIUS, WIDTH), (RADIUS, WIDTH)], [(WIDE, HEIGHT)], 10**8, 3 * 10**6, expo, pooled, got
    )
    before, after = exchange(top, bottom, "xy")
    (result,) = call(last_body, "last", [(HEIGHT, WIDTH)], [], 10**8, 10**6, before, turned, after)
    return (own, result)


def solution(mesh):
    return jax.shard_map(
        on_device,
        mesh=mesh,
        in_specs=(P("xy", "gz"), P(None, "gz", "xy", None), P("gz"), P("gz"), P()),
        out_specs=(P("xy", "gz"), P("xy", "gz")),
        check_vma=False,
    )
```

time: 196 us -> 65.9 us (0.34)
  matrix products: 68.3 us -> 0 us
  blocking collectives: 21.1 us -> 0 us
  loops' own time: 16.9 us -> 0 us
  starting transfers between devices: 50.6 us -> 37.6 us
  waiting for transfers between devices: 29.5 us -> 18.1 us
  Pallas kernels: 0 us -> 5.49 us
  local copies, waits for them, and re-layouts: 7.84 us -> 3.13 us
    dot_general x31 -> x0, matrix products: 68.3 us -> none  [the longest x8 32.6 us: cell_tensor(): jnp.dot(pooled_rows[:cells], offset_cols, precision=lax.Precision.HIGHEST)]
    all_to_all x1 -> x0, blocking collectives: 21.1 us -> none  [sum_at_owner(): lax.all_to_all(in_blocks(value, dim, count), axis, 0, 0, tiled=True)]
    another operation x1 -> x0, loops' own time: 16.9 us -> none  [pull_layers(): return lax.fori_loop(0, cotangent.shape[1], step, jnp.zeros_like(field))]
    all_to_all x1, waiting for transfers between devices: 16.7 us -> 0.01 us  [on_device(): got = lax.all_to_all(send, 'gz', 0, 0, tiled=True)]
    ppermute x8 -> x6, starting transfers between devices: 46.9 us -> 32.8 us  [exchange(): return (lax.ppermute(trailing, axis, up), lax.ppermute(leading, axis, down))]
    pallas_call x0 -> x5, Pallas kernels: none -> 5.49 us  [call(): pl.pallas_call(body, name=name, out_shape=[jax.ShapeDtypeStruct(shape, F3...]
    ppermute x8 -> x6, waiting for transfers between devices: 12.8 us -> 18.1 us  [exchange(): return (lax.ppermute(trailing, axis, up), lax.ppermute(leading, axis, down))]
    slice x7 -> x1, local copies, waits for them, and re-layouts: 3.41 us -> 0.01 us  [on_device(): before, after = exchange(density[:RADIUS], density[HEIGHT - RADIUS:], 'xy')]
  transfers between devices with their start and end apart: 9 -> 7, of which waited for: 8 -> 5; matrix products, arithmetic and copies ran while one was open for 1% -> 0% of each run, Pallas kernels for 0% -> 2%
where the time goes in v1:
time: 65.9 us; the launch traced here: 65.1 us
  starting transfers between devices  37.6 us (57%)
  waiting for transfers between devices  18.1 us (27%)
  Pallas kernels  5.49 us (8%)
  local copies, waits for them, and re-layouts  3.13 us (5%)
  between operations  0.73 us (1%)
    ppermute x6, starting transfers between devices, exchange(): return (lax.ppermute(trailing, axis, up), lax.ppermute(leading, axis, down))  32.8 us
    ppermute x6, waiting for transfers between devices, exchange(): return (lax.ppermute(trailing, axis, up), lax.ppermute(leading, axis, down))  18.1 us
    pallas_call x5, Pallas kernels, call(): pl.pallas_call(body, name=name, out_shape=[jax.ShapeDtypeStruct(shape, F3...  5.49 us
    all_to_all x1, starting transfers between devices, on_device(): got = lax.all_to_all(send, 'gz', 0, 0, tiled=True)  4.87 us
    unnamed x9, local copies, waits for them, and re-layouts  3.12 us
  transfers between devices with their start and end apart: 7, of which 5 were waited for; matrix products, arithmetic and copies ran while one was open for 0% of the time, Pallas kernels for 2%

profile of v1, /device:TPU:6, one launch (start us, length us, event | category | flops | bytes accessed | tf_op | source)
XLA Modules:
  0.0 65.1 jit_solution(5412594547407259421)
XLA Ops:
  0.6 0.0 copy-start
  0.6 0.8 %copy.7.eps = f32[4,2]{1,0:T(4,128)S(1)} copy(f32[4,2]{0,1:T(2,128)} %param.9) | data formatting | bytes 64 | tf_op args[4]
  1.4 1.0 %copy-done.1 = f32[6,4,16,256]{3,2,1,0:T(8,128)S(1)} copy-done((f32[6,4,16,256]{3,2,1,0:T(8,128)S(1)}, f32[6,4,16,256]{3,2,1,0:T(8,128)}, u32[]{:S(2)}) %copy-start.1) | copy-done | bytes 393240
  2.4 0.7 %copy-done.2 = s32[4]{0:T(128)S(1)} copy-done((s32[4]{0:T(128)S(1)}, s32[4]{0:T(128)}, u32[]{:S(2)}) %copy-start.2) | copy-done | bytes 40
  3.1 0.7 %copy-done.3 = s32[4]{0:T(128)S(1)} copy-done((s32[4]{0:T(128)S(1)}, s32[4]{0:T(128)}, u32[]{:S(2)}) %copy-start.3) | copy-done | bytes 40
  3.8 1.5 %pack.1 = f32[4,224,128]{2,1,0:T(8,128)} custom-call(s32[4]{0:T(128)S(1)} %copy-done.2, s32[4]{0:T(128)S(1)} %copy-done.3, f32[4,2]{1,0:T(4,128)S(1)} %copy.7.eps, f32[384,256]{1,0:T(8,128)S(1)} %bitcast.1), custom_call_target="tpu_custom_call" | custom-call | flops 1000000 | bytes 1000000 | tf_op jit(solution)/shard_map/pack/pallas_call | solution.py:57
  5.3 4.9 %all-to-all-start = ((f32[4,224,128]{2,1,0:T(8,128)}), f32[4,224,128]{2,1,0:T(8,128)S(1)}, u32[]{:S(2)}, u32[]{:S(2)}) async-start(f32[4,224,128]{2,1,0:T(8,128)} %pack.1), calls=%async_computation | async-start | bytes 917504 | tf_op jit(solution)/shard_map/all_to_all | solution.py:232
  10.1 14.5 %collective-permute-start.1 = (f32[32,512]{1,0:T(8,128)S(1)}, f32[32,512]{1,0:T(8,128)S(1)}, u32[]{:S(2)}, u32[]{:S(2)}) collective-permute-start(f32[32,512]{1,0:T(8,128)S(1)} %get-tuple-element.20), channel_id=1, source_target_pairs={{4,0},{8,4},{12,8},{16,12},{20,16},{24,20},{28,24},{32,28},{36,32}... | collective-permute-start | bytes 196616 | tf_op jit(solution)/shard_map/ppermute | solution.py:226
  24.7 1.9 %collective-permute-start = (f32[32,512]{1,0:T(8,128)S(1)}, f32[32,512]{1,0:T(8,128)S(1)}, u32[]{:S(2)}, u32[]{:S(2)}) collective-permute-start(f32[32,512]{1,0:T(8,128)S(1)} %get-tuple-element.21), channel_id=1, source_target_pairs={{0,4},{4,8},{8,12},{12,16},{16,20},{20,24},{24,28},{28,32},{32,36}... | collective-permute-start | bytes 196616 | tf_op jit(solution)/shard_map/ppermute | solution.py:226
  26.6 0.0 collective-permute-done.1.bottom
  26.6 11.6 %collective-permute-done.top = f32[32,512]{1,0:T(8,128)S(1)} collective-permute-done((f32[32,512]{1,0:T(8,128)S(1)}, f32[32,512]{1,0:T(8,128)S(1)}, u32[]{:S(2)}, u32[]{:S(2)}) %collective-permute-start) | collective-permute-done | bytes 65568 | tf_op jit(solution)/shard_map/ppermute | solution.py:226
  38.3 0.4 rows.1
  38.7 2.6 %collective-permute-start.2 = (f32[64,128]{1,0:T(8,128)S(1)}, f32[64,128]{1,0:T(8,128)S(1)}, u32[]{:S(2)}, u32[]{:S(2)}) collective-permute-start(f32[64,128]{1,0:T(8,128)S(1)} %get-tuple-element.11), channel_id=1, source_target_pairs={{0,1},{1,2},{2,3},{4,5},{5,6},{6,7},{8,9},{9,10},{10,11},{12,13},{... | collective-permute-start | bytes 98312 | tf_op jit(solution)/shard_map/ppermute | solution.py:226
  41.2 1.3 %collective-permute-start.3 = (f32[64,128]{1,0:T(8,128)S(1)}, f32[64,128]{1,0:T(8,128)S(1)}, u32[]{:S(2)}, u32[]{:S(2)}) collective-permute-start(f32[64,128]{1,0:T(8,128)S(1)} %get-tuple-element.13), channel_id=1, source_target_pairs={{1,0},{2,1},{3,2},{5,4},{6,5},{7,6},{9,8},{10,9},{11,10},{13,12},{... | collective-permute-start | bytes 98312 | tf_op jit(solution)/shard_map/ppermute | solution.py:226
  42.5 0.3 collective-permute-done.2.left
  42.8 4.3 %collective-permute-done.3.right = f32[64,128]{1,0:T(8,128)S(1)} collective-permute-done((f32[64,128]{1,0:T(8,128)S(1)}, f32[64,128]{1,0:T(8,128)S(1)}, u32[]{:S(2)}, u32[]{:S(2)}) %collective-permute-start.3) | collective-permute-done | bytes 32800 | tf_op jit(solution)/shard_map/ppermute | solution.py:226
  47.1 0.8 %forward.1 = (f32[8,72,128]{2,1,0:T(8,128)S(1)}, f32[1088,256]{1,0:T(8,128)S(1)}) custom-call(f32[64,128]{1,0:T(8,128)S(1)} %collective-permute-done.2.left, f32[512,128]{1,0:T(8,128)S(1)} %get-tuple-element.12.own, f32[64,128]{1,0:T(8,128)S(1)} %collective-permute-done.3.right), custom_call_target="tpu_custom_call" | custom-call | flops 100000000 | bytes 2000000 | tf_op jit(solution)/shard_map/forward/pallas_call | solution.py:57
  47.9 0.0 all-to-all-done.got
  48.0 1.8 %backward.1 = (f32[128,512]{1,0:T(8,128)}, f32[128,512]{1,0:T(8,128)S(1)}, f32[32,512]{1,0:T(8,128)S(1)}, f32[32,512]{1,0:T(8,128)S(1)}) custom-call(f32[8,72,128]{2,1,0:T(8,128)S(1)} %get-tuple-element.14.expo, f32[1088,256]{1,0:T(8,128)S(1)} %get-tuple-element.15.pooled, f32[4,224,128]{2,1,0:T(8,128)S(1)} %all-to-all-done.got), custom_call_target="tpu_custom_call" | custom-call | flops 100000000 | bytes 3000000 | tf_op jit(solution)/shard_map/backward/pallas_call | solution.py:57
  49.8 1.9 %collective-permute-start.4 = (f32[32,512]{1,0:T(8,128)S(1)}, f32[32,512]{1,0:T(8,128)S(1)}, u32[]{:S(2)}, u32[]{:S(2)}) collective-permute-start(f32[32,512]{1,0:T(8,128)S(1)} %get-tuple-element.17), channel_id=1, source_target_pairs={{0,4},{4,8},{8,12},{12,16},{16,20},{20,24},{24,28},{28,32},{32,36}... | collective-permute-start | bytes 196616 | tf_op jit(solution)/shard_map/ppermute | solution.py:226
  51.7 10.6 %collective-permute-start.5 = (f32[32,512]{1,0:T(8,128)S(1)}, f32[32,512]{1,0:T(8,128)S(1)}, u32[]{:S(2)}, u32[]{:S(2)}) collective-permute-start(f32[32,512]{1,0:T(8,128)S(1)} %get-tuple-element.19), channel_id=1, source_target_pairs={{4,0},{8,4},{12,8},{16,12},{20,16},{24,20},{28,24},{32,28},{36,32}... | collective-permute-start | bytes 196616 | tf_op jit(solution)/shard_map/ppermute | solution.py:226
  62.3 0.3 collective-permute-done.4.top
  62.6 1.6 %collective-permute-done.5.bottom = f32[32,512]{1,0:T(8,128)S(1)} collective-permute-done((f32[32,512]{1,0:T(8,128)S(1)}, f32[32,512]{1,0:T(8,128)S(1)}, u32[]{:S(2)}, u32[]{:S(2)}) %collective-permute-start.5) | collective-permute-done | bytes 65568 | tf_op jit(solution)/shard_map/ppermute | solution.py:226
  64.2 0.9 %last.1 = f32[128,512]{1,0:T(8,128)} custom-call(f32[32,512]{1,0:T(8,128)S(1)} %collective-permute-done.4.top, f32[128,512]{1,0:T(8,128)S(1)} %get-tuple-element.18.own, f32[32,512]{1,0:T(8,128)S(1)} %collective-permute-done.5.bottom), custom_call_target="tpu_custom_call" | custom-call | flops 100000000 | bytes 1000000 | tf_op jit(solution)/shard_map/last/pallas_call | solution.py:57
  (5 shorter events, 0.0 us)
Async XLA Ops:
  0.6 9.5 %copy-start = (f32[128,512]{1,0:T(8,128)S(1)}, f32[128,512]{1,0:T(8,128)}, u32[]{:S(2)}) copy-start(f32[128,512]{1,0:T(8,128)} %own.1) | copy-start | bytes 786436
  1.4 1.0 %copy-start.1 = (f32[6,4,16,256]{3,2,1,0:T(8,128)S(1)}, f32[6,4,16,256]{3,2,1,0:T(8,128)}, u32[]{:S(2)}) copy-start(f32[6,4,16,256]{3,2,1,0:T(8,128)} %param.6) | copy-start | bytes 1179652
  2.4 0.7 %copy-start.2 = (s32[4]{0:T(128)S(1)}, s32[4]{0:T(128)}, u32[]{:S(2)}) copy-start(s32[4]{0:T(128)} %slope.1) | copy-start | bytes 52
  3.1 0.7 %copy-start.3 = (s32[4]{0:T(128)S(1)}, s32[4]{0:T(128)}, u32[]{:S(2)}) copy-start(s32[4]{0:T(128)} %block.1) | copy-start | bytes 52
  5.3 42.7 %all-to-all-start = ((f32[4,224,128]{2,1,0:T(8,128)}), f32[4,224,128]{2,1,0:T(8,128)S(1)}, u32[]{:S(2)}, u32[]{:S(2)}) async-start(f32[4,224,128]{2,1,0:T(8,128)} %pack.1), calls=%async_computation | async-start | bytes 917504 | tf_op jit(solution)/shard_map/all_to_all | solution.py:232
  10.1 16.5 %collective-permute-start.1 = (f32[32,512]{1,0:T(8,128)S(1)}, f32[32,512]{1,0:T(8,128)S(1)}, u32[]{:S(2)}, u32[]{:S(2)}) collective-permute-start(f32[32,512]{1,0:T(8,128)S(1)} %get-tuple-element.20), channel_id=1, source_target_pairs={{4,0},{8,4},{12,8},{16,12},{20,16},{24,20},{28,24},{32,28},{36,32}... | collective-permute-start | bytes 196616 | tf_op jit(solution)/shard_map/ppermute | solution.py:226
  24.7 13.6 %collective-permute-start = (f32[32,512]{1,0:T(8,128)S(1)}, f32[32,512]{1,0:T(8,128)S(1)}, u32[]{:S(2)}, u32[]{:S(2)}) collective-permute-start(f32[32,512]{1,0:T(8,128)S(1)} %get-tuple-element.21), channel_id=1, source_target_pairs={{0,4},{4,8},{8,12},{12,16},{16,20},{20,24},{24,28},{28,32},{32,36}... | collective-permute-start | bytes 196616 | tf_op jit(solution)/shard_map/ppermute | solution.py:226
  38.7 4.1 %collective-permute-start.2 = (f32[64,128]{1,0:T(8,128)S(1)}, f32[64,128]{1,0:T(8,128)S(1)}, u32[]{:S(2)}, u32[]{:S(2)}) collective-permute-start(f32[64,128]{1,0:T(8,128)S(1)} %get-tuple-element.11), channel_id=1, source_target_pairs={{0,1},{1,2},{2,3},{4,5},{5,6},{6,7},{8,9},{9,10},{10,11},{12,13},{... | collective-permute-start | bytes 98312 | tf_op jit(solution)/shard_map/ppermute | solution.py:226
  41.2 5.9 %collective-permute-start.3 = (f32[64,128]{1,0:T(8,128)S(1)}, f32[64,128]{1,0:T(8,128)S(1)}, u32[]{:S(2)}, u32[]{:S(2)}) collective-permute-start(f32[64,128]{1,0:T(8,128)S(1)} %get-tuple-element.13), channel_id=1, source_target_pairs={{1,0},{2,1},{3,2},{5,4},{6,5},{7,6},{9,8},{10,9},{11,10},{13,12},{... | collective-permute-start | bytes 98312 | tf_op jit(solution)/shard_map/ppermute | solution.py:226
  49.8 12.8 %collective-permute-start.4 = (f32[32,512]{1,0:T(8,128)S(1)}, f32[32,512]{1,0:T(8,128)S(1)}, u32[]{:S(2)}, u32[]{:S(2)}) collective-permute-start(f32[32,512]{1,0:T(8,128)S(1)} %get-tuple-element.17), channel_id=1, source_target_pairs={{0,4},{4,8},{8,12},{12,16},{16,20},{20,24},{24,28},{28,32},{32,36}... | collective-permute-start | bytes 196616 | tf_op jit(solution)/shard_map/ppermute | solution.py:226
  51.7 12.4 %collective-permute-start.5 = (f32[32,512]{1,0:T(8,128)S(1)}, f32[32,512]{1,0:T(8,128)S(1)}, u32[]{:S(2)}, u32[]{:S(2)}) collective-permute-start(f32[32,512]{1,0:T(8,128)S(1)} %get-tuple-element.19), channel_id=1, source_target_pairs={{4,0},{8,4},{12,8},{16,12},{20,16},{24,20},{28,24},{32,28},{36,32}... | collective-permute-start | bytes 196616 | tf_op jit(solution)/shard_map/ppermute | solution.py:226

commit v2 on v1

--- a/solution.py
+++ b/solution.py
@@ -1,4 +1,3 @@
-import functools
 import math
 
 import jax
@@ -10,7 +9,6 @@
 
 SUB = 8
 RADIUS = 32
-MATS = 4
 SLOPES = 5
 SCALE = 1.0 / float((RADIUS + 1) ** 2)
 BF = jnp.bfloat16
@@ -53,10 +51,9 @@
     return (iota((1, HEIGHT), 1) % SUB).astype(F32) - 3.5
 
 
-def call(body, name, outs, scratch, flops, moved, *args, smem=()):
+def call(body, outs, scratch, flops, moved, *args, smem=()):
     return pl.pallas_call(
         body,
-        name=name,
         out_shape=[jax.ShapeDtypeStruct(shape, F32) for shape in outs],
         in_specs=[SMEM if index in smem else VMEM for index in range(len(args))],
         out_specs=[VMEM for _ in outs],
@@ -66,10 +63,21 @@
     )(*args)
 
 
-def pack_body(slope, block, eps, cot, send):
+def pack_body(slope_hbm, block_hbm, eps_hbm, cot_hbm, send, slope, block, eps, cot, sems):
+    small = [
+        pltpu.make_async_copy(source, target, sems.at[3 + index])
+        for index, (source, target) in enumerate([(slope_hbm, slope), (block_hbm, block), (eps_hbm, eps)])
+    ]
+    slabs = [
+        pltpu.make_async_copy(cot_hbm.at[pl.ds(128 * slab, 128)], cot.at[pl.ds(128 * slab, 128)], sems.at[slab])
+        for slab in range(3)
+    ]
+    for copy in slabs + small:
+        copy.start()
     low = iota((SUB, HEIGHT), 0) < 4
     zero = jnp.zeros((SUB, HEIGHT), F32)
     for slab in range(3):
+        slabs[slab].wait()
         turned = cot[slab * 128 : slab * 128 + 128, :].T
         for owner in range(4):
             first, base = (64 * owner, 72 * slab)
@@ -77,12 +85,14 @@
             after = zero if owner == 3 else turned[first + 64 : first + 72]
             before = zero if owner == 0 else turned[first - 8 : first]
             send[owner, base + 64 : base + 72, :] = jnp.where(low, after, before)
+    for copy in small:
+        copy.wait()
     layer = (iota((SUB, HEIGHT), 1) % 64) // 16
     row = iota((SUB, HEIGHT), 0)
     table = zero
     for index in range(4):
-        one = eps[block[index], 0]
-        two = eps[block[index], 1]
+        one = eps[0, block[index]]
+        two = eps[1, block[index]]
         level = slope[index].astype(F32)
         column = jnp.where(row == 0, level, jnp.where(row == 1, one, jnp.where(row == 2, two, 0.0)))
         table = jnp.where(layer == index, column, table)
@@ -90,8 +100,17 @@
         send[owner, 216:224, :] = table
 
 
-def rows_body(top, own, bottom, out, first, last):
-    padded = jnp.concatenate([top[...], own[...], bottom[...]], axis=0)
+def odd(axis):
+    return lax.rem(lax.axis_index(axis), 2) == 1
+
+
+def sides(axis, near, far):
+    return (jnp.where(odd(axis), near, far), jnp.where(odd(axis), far, near))
+
+
+def rows_body(near, own, far, out, to_near, to_far):
+    before, after = sides("xy", near[...], far[...])
+    padded = jnp.concatenate([before, own[...], after], axis=0)
     matrix = band(HEIGHT, HEIGHT + 2 * RADIUS)
     total = None
     for part in parts_of(padded, 3):
@@ -99,12 +118,12 @@
         total = term if total is None else total + term
     turned = (total * SCALE).T
     out[...] = turned
-    first[...] = turned[:64]
-    last[...] = turned[WIDTH - 64 :]
-
-
-def forward_body(left, own, right, expo, pooled, natural):
-    padded = jnp.concatenate([left[...], own[...], right[...]], axis=0)
+    to_near[...], to_far[...] = sides("gz", turned[:64], turned[WIDTH - 64 :])
+
+
+def forward_body(near, own, far, expo, pooled, natural):
+    left, right = sides("gz", near[...], far[...])
+    padded = jnp.concatenate([left, own[...], right], axis=0)
     padded = jnp.concatenate(parts_of(padded, 3), axis=1)
     matrix = band(192, 256)
     for block in range(3):
@@ -135,8 +154,9 @@
     pooled[...] = dot(rows, base) * (1.0 / 64.0)
 
 
-def backward_body(expo, pooled, got, out, turned, top, bottom, natural):
+def backward_body(expo, pooled, got, out, turned, to_near, to_far, natural):
     half = iota((1, 128), 1) < 64
+
     def pair(a, b):
         return jnp.where(half, a, b)
 
@@ -208,43 +228,86 @@
         pieces.append((wide[:, :128] + wide[:, 128:]) * SCALE)
     result = jnp.concatenate(pieces, axis=0).T
     turned[...] = result
-    top[...] = result[:RADIUS]
-    bottom[...] = result[HEIGHT - RADIUS :]
-
-
-def last_body(top, own, bottom, out):
-    padded = jnp.concatenate([top[...], own[...], bottom[...]], axis=0)
+    to_near[...], to_far[...] = sides("xy", result[:RADIUS], result[HEIGHT - RADIUS :])
+
+
+def last_body(near, own, far, out):
+    before, after = sides("xy", near[...], far[...])
+    padded = jnp.concatenate([before, own[...], after], axis=0)
     matrix = band(HEIGHT, HEIGHT + 2 * RADIUS)
     high, low = parts_of(padded, 2)
     out[...] = (dot(matrix, high) + dot(matrix, low)) * SCALE
 
 
-def exchange(leading, trailing, axis):
+def swap(near, far, axis):
     count = lax.axis_size(axis)
-    up = [(i, i + 1) for i in range(count - 1)]
-    down = [(j, i) for i, j in up]
-    return (lax.ppermute(trailing, axis, up), lax.ppermute(leading, axis, down))
-
-
-def on_device(density, cotangent, slope, layer_block, block_eps):
-    flat = cotangent.reshape(384, 256)
-    (send,) = call(pack_body, "pack", [(4, ROWS, 128)], [], 10**6, 10**6, slope, layer_block, block_eps, flat, smem=(0, 1, 2))
+
+    def pairs(start):
+        return [p for i in range(start, count - 1, 2) for p in ((i, i + 1), (i + 1, i))]
+
+    far = lax.ppermute(far, axis, pairs(1))
+    near = lax.ppermute(near, axis, pairs(0))
+    return (near, far)
+
+
+def edges_body(density, near, far, sems):
+    first = jnp.where(odd("xy"), 0, HEIGHT - RADIUS)
+    second = HEIGHT - RADIUS - first
+    copies = [
+        pltpu.make_async_copy(density.at[pl.ds(pl.multiple_of(start, RADIUS), RADIUS)], target, sems.at[index])
+        for index, (start, target) in enumerate([(first, near), (second, far)])
+    ]
+    for copy in copies:
+        copy.start()
+    for copy in copies:
+        copy.wait()
+
+
+def steps(density, cotangent, slope, layer_block, block_eps):
+    near, far = pl.pallas_call(
+        edges_body,
+        name="edges",
+        out_shape=[jax.ShapeDtypeStruct((RADIUS, WIDTH), F32)] * 2,
+        in_specs=[pl.BlockSpec(memory_space=pltpu.HBM)],
+        out_specs=[VMEM] * 2,
+        scratch_shapes=[pltpu.SemaphoreType.DMA((2,))],
+        compiler_params=pltpu.CompilerParams(vmem_limit_bytes=60 * 1024 * 1024),
+        cost_estimate=pl.CostEstimate(flops=10**5, bytes_accessed=10**6, transcendentals=0),
+    )(density)
+    near, far = swap(near, far, "xy")
+    (send,) = pl.pallas_call(
+        pack_body,
+        name="pack",
+        out_shape=[jax.ShapeDtypeStruct((4, ROWS, 128), F32)],
+        in_specs=[pl.BlockSpec(memory_space=pltpu.HBM)] * 4,
+        out_specs=[VMEM],
+        scratch_shapes=[
+            pltpu.SMEM((4,), jnp.int32),
+            pltpu.SMEM((4,), jnp.int32),
+            pltpu.SMEM((2, 4), F32),
+            pltpu.VMEM((384, 256), F32),
+            pltpu.SemaphoreType.DMA((6,)),
+        ],
+        compiler_params=pltpu.CompilerParams(vmem_limit_bytes=60 * 1024 * 1024),
+        cost_estimate=pl.CostEstimate(flops=10**6, bytes_accessed=10**6, transcendentals=0),
+    )(slope, layer_block, block_eps.T, cotangent.reshape(384, 256))
     got = lax.all_to_all(send, "gz", 0, 0, tiled=True)
-    before, after = exchange(density[:RADIUS], density[HEIGHT - RADIUS :], "xy")
-    across, first, last = call(rows_body, "rows", [(WIDTH, HEIGHT), (64, HEIGHT), (64, HEIGHT)], [], 10**8, 10**6, before, density, after)
-    left, right = exchange(first, last, "gz")
-    expo, pooled = call(forward_body, "forward", [(SUB, CELLS, HEIGHT), (1088, 256)], [(WIDE, HEIGHT)], 10**8, 2 * 10**6, left, across, right)
-    own, turned, top, bottom = call(
-        backward_body, "backward", [(HEIGHT, WIDTH), (HEIGHT, WIDTH), (RADIUS, WIDTH), (RADIUS, WIDTH)], [(WIDE, HEIGHT)], 10**8, 3 * 10**6, expo, pooled, got
+    across, near, far = (
+        *call(rows_body, [(WIDTH, HEIGHT), (64, HEIGHT), (64, HEIGHT)], [], 10**8, 10**6, near, density, far),
     )
-    before, after = exchange(top, bottom, "xy")
-    (result,) = call(last_body, "last", [(HEIGHT, WIDTH)], [], 10**8, 10**6, before, turned, after)
+    near, far = swap(near, far, "gz")
+    expo, pooled = call(forward_body, [(SUB, CELLS, HEIGHT), (1088, 256)], [(WIDE, HEIGHT)], 10**8, 2 * 10**6, near, across, far)
+    own, turned, near, far = call(
+        backward_body, [(HEIGHT, WIDTH), (HEIGHT, WIDTH), (RADIUS, WIDTH), (RADIUS, WIDTH)], [(WIDE, HEIGHT)], 10**8, 3 * 10**6, expo, pooled, got
+    )
+    near, far = swap(near, far, "xy")
+    (result,) = call(last_body, [(HEIGHT, WIDTH)], [], 10**8, 10**6, near, turned, far)
     return (own, result)
 
 
 def solution(mesh):
     return jax.shard_map(
-        on_device,
+        steps,
         mesh=mesh,
         in_specs=(P("xy", "gz"), P(None, "gz", "xy", None), P("gz"), P("gz"), P()),
         out_specs=(P("xy", "gz"), P("xy", "gz")),

time: 65.9 us -> 58.2 us (0.88)
  the two profiles are of different devices: /device:TPU:6 before, /device:TPU:22 now
where the time goes in v2:
time: 58.2 us; the launch traced here: 57.9 us
  starting transfers between devices  38 us (65%)
  waiting for transfers between devices  11.3 us (19%)
  Pallas kernels  7.71 us (13%)
  between operations  0.75 us (1%)
    ppermute x3, starting transfers between devices, swap(): far = lax.ppermute(far, axis, pairs(1))  24.8 us
    ppermute x3, waiting for transfers between devices, swap(): far = lax.ppermute(far, axis, pairs(1))  11.3 us
    ppermute x3, starting transfers between devices, swap(): near = lax.ppermute(near, axis, pairs(0))  8.05 us
    all_to_all x1, starting transfers between devices, steps(): got = lax.all_to_all(send, 'gz', 0, 0, tiled=True)  5.22 us
    pallas_call x4, Pallas kernels, call(): pl.pallas_call(body, out_shape=[jax.ShapeDtypeStruct(shape, F32) for shap...  4.04 us
    pallas_call x1, Pallas kernels, steps(): pl.pallas_call(pack_body, name='pack', out_shape=[jax.ShapeDtypeStruct((4...  2.13 us
    pallas_call x1, Pallas kernels, steps(): pl.pallas_call(edges_body, name='edges', out_shape=[jax.ShapeDtypeStruct(...  1.54 us
  transfers between devices with their start and end apart: 7, of which 3 were waited for; matrix products, arithmetic and copies ran while one was open for 0% of the time, Pallas kernels for 5%

profile of v2, /device:TPU:22, one launch (start us, length us, event | category | flops | bytes accessed | tf_op | source)
XLA Modules:
  0.0 57.9 jit_solution(15256280946572322124)
XLA Ops:
  0.6 0.0 copy-start
  0.6 2.1 %pack.1 = f32[4,224,128]{2,1,0:T(8,128)} custom-call(s32[4]{0:T(128)} %slope_hbm.1, s32[4]{0:T(128)} %block_hbm.1, f32[2,4]{1,0:T(2,128)} %bitcast.3, f32[384,256]{1,0:T(8,128)} %bitcast.2), custom_call_target="tpu_custom_call" | custom-call | flops 1000000 | bytes 1000000 | tf_op jit(solution)/shard_map/pack/pallas_call | solution.py:278
  2.8 5.2 %all-to-all-start = ((f32[4,224,128]{2,1,0:T(8,128)}), f32[4,224,128]{2,1,0:T(8,128)S(1)}, u32[]{:S(2)}, u32[]{:S(2)}) async-start(f32[4,224,128]{2,1,0:T(8,128)} %pack.1), calls=%async_computation | async-start | bytes 917504 | tf_op jit(solution)/shard_map/all_to_all | solution.py:294
  8.0 1.5 %edges.1 = (f32[32,512]{1,0:T(8,128)}, f32[32,512]{1,0:T(8,128)}) custom-call(f32[128,512]{1,0:T(8,128)} %own.1), custom_call_target="tpu_custom_call" | custom-call | flops 100000 | bytes 1000000 | tf_op jit(solution)/shard_map/edges/pallas_call | solution.py:267
  9.5 1.9 %collective-permute-start = (f32[32,512]{1,0:T(8,128)}, f32[32,512]{1,0:T(8,128)S(1)}, u32[]{:S(2)}, u32[]{:S(2)}) collective-permute-start(f32[32,512]{1,0:T(8,128)} %get-tuple-element.13), channel_id=1, source_target_pairs={{0,4},{4,0},{8,12},{12,8},{16,20},{20,16},{24,28},{28,24},{32,36},... | collective-permute-start | bytes 196616 | tf_op jit(solution)/shard_map/ppermute | solution.py:249
  11.5 15.1 %collective-permute-start.1 = (f32[32,512]{1,0:T(8,128)}, f32[32,512]{1,0:T(8,128)S(1)}, u32[]{:S(2)}, u32[]{:S(2)}) collective-permute-start(f32[32,512]{1,0:T(8,128)} %get-tuple-element.14), channel_id=1, source_target_pairs={{4,8},{8,4},{12,16},{16,12},{20,24},{24,20},{28,32},{32,28},{36,40... | collective-permute-start | bytes 196616 | tf_op jit(solution)/shard_map/ppermute | solution.py:248
  26.6 0.0 collective-permute-done.near
  26.6 2.7 %collective-permute-done.1.far = f32[32,512]{1,0:T(8,128)S(1)} collective-permute-done((f32[32,512]{1,0:T(8,128)}, f32[32,512]{1,0:T(8,128)S(1)}, u32[]{:S(2)}, u32[]{:S(2)}) %collective-permute-start.1) | collective-permute-done | bytes 65568 | tf_op jit(solution)/shard_map/ppermute | solution.py:248
  29.3 0.0 copy-done
  29.3 0.4 shard_map.68
  29.7 4.2 %collective-permute-start.2 = (f32[64,128]{1,0:T(8,128)S(1)}, f32[64,128]{1,0:T(8,128)S(1)}, u32[]{:S(2)}, u32[]{:S(2)}) collective-permute-start(f32[64,128]{1,0:T(8,128)S(1)} %get-tuple-element.15), channel_id=1, source_target_pairs={{0,1},{1,0},{2,3},{3,2},{4,5},{5,4},{6,7},{7,6},{8,9},{9,8},{10,11... | collective-permute-start | bytes 98312 | tf_op jit(solution)/shard_map/ppermute | solution.py:249
  34.0 1.9 %collective-permute-start.3 = (f32[64,128]{1,0:T(8,128)S(1)}, f32[64,128]{1,0:T(8,128)S(1)}, u32[]{:S(2)}, u32[]{:S(2)}) collective-permute-start(f32[64,128]{1,0:T(8,128)S(1)} %get-tuple-element.17), channel_id=1, source_target_pairs={{1,2},{2,1},{5,6},{6,5},{9,10},{10,9},{13,14},{14,13},{17,18},{18,... | collective-permute-start | bytes 98312 | tf_op jit(solution)/shard_map/ppermute | solution.py:248
  35.9 0.0 collective-permute-done.2.near
  35.9 3.9 %collective-permute-done.3.far = f32[64,128]{1,0:T(8,128)S(1)} collective-permute-done((f32[64,128]{1,0:T(8,128)S(1)}, f32[64,128]{1,0:T(8,128)S(1)}, u32[]{:S(2)}, u32[]{:S(2)}) %collective-permute-start.3) | collective-permute-done | bytes 32800 | tf_op jit(solution)/shard_map/ppermute | solution.py:248
  39.8 0.8 %shard_map.69 = (f32[8,72,128]{2,1,0:T(8,128)S(1)}, f32[1088,256]{1,0:T(8,128)S(1)}) custom-call(f32[64,128]{1,0:T(8,128)S(1)} %collective-permute-done.2.near, f32[512,128]{1,0:T(8,128)S(1)} %get-tuple-element.16.own, f32[64,128]{1,0:T(8,128)S(1)} %collective-permute-done.3.far), custom_call_target="tpu_custom_call" | custom-call | flops 100000000 | bytes 2000000 | tf_op jit(solution)/shard_map/pallas_call | solution.py:55
  40.6 0.0 all-to-all-done.got
  40.6 1.9 %shard_map.70 = (f32[128,512]{1,0:T(8,128)}, f32[128,512]{1,0:T(8,128)S(1)}, f32[32,512]{1,0:T(8,128)S(1)}, f32[32,512]{1,0:T(8,128)S(1)}) custom-call(f32[8,72,128]{2,1,0:T(8,128)S(1)} %get-tuple-element.18.expo, f32[1088,256]{1,0:T(8,128)S(1)} %get-tuple-element.19.pooled, f32[4,224,128]{2,1,0:T(8,128)S(1)} %all-to-all-done.got), custom_call_target="tpu_custom_call" | custom-call | flops 100000000 | bytes 3000000 | tf_op jit(solution)/shard_map/pallas_call | solution.py:55
  42.5 1.9 %collective-permute-start.4 = (f32[32,512]{1,0:T(8,128)S(1)}, f32[32,512]{1,0:T(8,128)S(1)}, u32[]{:S(2)}, u32[]{:S(2)}) collective-permute-start(f32[32,512]{1,0:T(8,128)S(1)} %get-tuple-element.21), channel_id=1, source_target_pairs={{0,4},{4,0},{8,12},{12,8},{16,20},{20,16},{24,28},{28,24},{32,36},... | collective-permute-start | bytes 196616 | tf_op jit(solution)/shard_map/ppermute | solution.py:249
  44.4 7.7 %collective-permute-start.5 = (f32[32,512]{1,0:T(8,128)S(1)}, f32[32,512]{1,0:T(8,128)S(1)}, u32[]{:S(2)}, u32[]{:S(2)}) collective-permute-start(f32[32,512]{1,0:T(8,128)S(1)} %get-tuple-element.23), channel_id=1, source_target_pairs={{4,8},{8,4},{12,16},{16,12},{20,24},{24,20},{28,32},{32,28},{36,40... | collective-permute-start | bytes 196616 | tf_op jit(solution)/shard_map/ppermute | solution.py:248
  52.1 0.0 collective-permute-done.4.near
  52.1 4.8 %collective-permute-done.5.far = f32[32,512]{1,0:T(8,128)S(1)} collective-permute-done((f32[32,512]{1,0:T(8,128)S(1)}, f32[32,512]{1,0:T(8,128)S(1)}, u32[]{:S(2)}, u32[]{:S(2)}) %collective-permute-start.5) | collective-permute-done | bytes 65568 | tf_op jit(solution)/shard_map/ppermute | solution.py:248
  56.9 1.0 %shard_map.71 = f32[128,512]{1,0:T(8,128)} custom-call(f32[32,512]{1,0:T(8,128)S(1)} %collective-permute-done.4.near, f32[128,512]{1,0:T(8,128)S(1)} %get-tuple-element.22.own, f32[32,512]{1,0:T(8,128)S(1)} %collective-permute-done.5.far), custom_call_target="tpu_custom_call" | custom-call | flops 100000000 | bytes 1000000 | tf_op jit(solution)/shard_map/pallas_call | solution.py:55
Async XLA Ops:
  0.6 28.7 %copy-start = (f32[128,512]{1,0:T(8,128)S(1)}, f32[128,512]{1,0:T(8,128)}, u32[]{:S(2)}) copy-start(f32[128,512]{1,0:T(8,128)} %own.1) | copy-start | bytes 786436
  2.8 37.8 %all-to-all-start = ((f32[4,224,128]{2,1,0:T(8,128)}), f32[4,224,128]{2,1,0:T(8,128)S(1)}, u32[]{:S(2)}, u32[]{:S(2)}) async-start(f32[4,224,128]{2,1,0:T(8,128)} %pack.1), calls=%async_computation | async-start | bytes 917504 | tf_op jit(solution)/shard_map/all_to_all | solution.py:294
  9.5 17.1 %collective-permute-start = (f32[32,512]{1,0:T(8,128)}, f32[32,512]{1,0:T(8,128)S(1)}, u32[]{:S(2)}, u32[]{:S(2)}) collective-permute-start(f32[32,512]{1,0:T(8,128)} %get-tuple-element.13), channel_id=1, source_target_pairs={{0,4},{4,0},{8,12},{12,8},{16,20},{20,16},{24,28},{28,24},{32,36},... | collective-permute-start | bytes 196616 | tf_op jit(solution)/shard_map/ppermute | solution.py:249
  11.5 17.9 %collective-permute-start.1 = (f32[32,512]{1,0:T(8,128)}, f32[32,512]{1,0:T(8,128)S(1)}, u32[]{:S(2)}, u32[]{:S(2)}) collective-permute-start(f32[32,512]{1,0:T(8,128)} %get-tuple-element.14), channel_id=1, source_target_pairs={{4,8},{8,4},{12,16},{16,12},{20,24},{24,20},{28,32},{32,28},{36,40... | collective-permute-start | bytes 196616 | tf_op jit(solution)/shard_map/ppermute | solution.py:248
  29.7 6.2 %collective-permute-start.2 = (f32[64,128]{1,0:T(8,128)S(1)}, f32[64,128]{1,0:T(8,128)S(1)}, u32[]{:S(2)}, u32[]{:S(2)}) collective-permute-start(f32[64,128]{1,0:T(8,128)S(1)} %get-tuple-element.15), channel_id=1, source_target_pairs={{0,1},{1,0},{2,3},{3,2},{4,5},{5,4},{6,7},{7,6},{8,9},{9,8},{10,11... | collective-permute-start | bytes 98312 | tf_op jit(solution)/shard_map/ppermute | solution.py:249
  34.0 5.8 %collective-permute-start.3 = (f32[64,128]{1,0:T(8,128)S(1)}, f32[64,128]{1,0:T(8,128)S(1)}, u32[]{:S(2)}, u32[]{:S(2)}) collective-permute-start(f32[64,128]{1,0:T(8,128)S(1)} %get-tuple-element.17), channel_id=1, source_target_pairs={{1,2},{2,1},{5,6},{6,5},{9,10},{10,9},{13,14},{14,13},{17,18},{18,... | collective-permute-start | bytes 98312 | tf_op jit(solution)/shard_map/ppermute | solution.py:248
  42.5 9.6 %collective-permute-start.4 = (f32[32,512]{1,0:T(8,128)S(1)}, f32[32,512]{1,0:T(8,128)S(1)}, u32[]{:S(2)}, u32[]{:S(2)}) collective-permute-start(f32[32,512]{1,0:T(8,128)S(1)} %get-tuple-element.21), channel_id=1, source_target_pairs={{0,4},{4,0},{8,12},{12,8},{16,20},{20,16},{24,28},{28,24},{32,36},... | collective-permute-start | bytes 196616 | tf_op jit(solution)/shard_map/ppermute | solution.py:249
  44.4 12.5 %collective-permute-start.5 = (f32[32,512]{1,0:T(8,128)S(1)}, f32[32,512]{1,0:T(8,128)S(1)}, u32[]{:S(2)}, u32[]{:S(2)}) collective-permute-start(f32[32,512]{1,0:T(8,128)S(1)} %get-tuple-element.23), channel_id=1, source_target_pairs={{4,8},{8,4},{12,16},{16,12},{20,24},{24,20},{28,32},{32,28},{36,40... | collective-permute-start | bytes 196616 | tf_op jit(solution)/shard_map/ppermute | solution.py:248

commit v3 on v2

--- a/solution.py
+++ b/solution.py
@@ -15,6 +15,7 @@
 F32 = jnp.float32
 VMEM = pl.BlockSpec(memory_space=pltpu.VMEM)
 SMEM = pl.BlockSpec(memory_space=pltpu.SMEM)
+HBM = pl.BlockSpec(memory_space=pltpu.HBM)
 LIMIT = 24 << 20
 
 HEIGHT = 128
@@ -63,7 +64,7 @@
     )(*args)
 
 
-def pack_body(slope_hbm, block_hbm, eps_hbm, cot_hbm, send, slope, block, eps, cot, sems):
+def pack_body(slope_hbm, block_hbm, eps_hbm, cot_hbm, send_hbm, slope, block, eps, cot, send, sems):
     small = [
         pltpu.make_async_copy(source, target, sems.at[3 + index])
         for index, (source, target) in enumerate([(slope_hbm, slope), (block_hbm, block), (eps_hbm, eps)])
@@ -76,6 +77,15 @@
         copy.start()
     low = iota((SUB, HEIGHT), 0) < 4
     zero = jnp.zeros((SUB, HEIGHT), F32)
+    outs = []
+
+    def put(first, rows):
+        copy = pltpu.make_async_copy(
+            send.at[:, pl.ds(first, rows)], send_hbm.at[:, pl.ds(first, rows)], sems.at[6 + len(outs)]
+        )
+        copy.start()
+        outs.append(copy)
+
     for slab in range(3):
         slabs[slab].wait()
         turned = cot[slab * 128 : slab * 128 + 128, :].T
@@ -85,6 +95,8 @@
             after = zero if owner == 3 else turned[first + 64 : first + 72]
             before = zero if owner == 0 else turned[first - 8 : first]
             send[owner, base + 64 : base + 72, :] = jnp.where(low, after, before)
+        if slab < 2:
+            put(72 * slab, 72)
     for copy in small:
         copy.wait()
     layer = (iota((SUB, HEIGHT), 1) % 64) // 16
@@ -98,6 +110,9 @@
         table = jnp.where(layer == index, column, table)
     for owner in range(4):
         send[owner, 216:224, :] = table
+    put(144, 80)
+    for copy in outs:
+        copy.wait()
 
 
 def odd(axis):
@@ -108,22 +123,39 @@
     return (jnp.where(odd(axis), near, far), jnp.where(odd(axis), far, near))
 
 
-def rows_body(near, own, far, out, to_near, to_far):
+def low_lanes():
+    return iota((1, 128), 1) < 64
+
+
+def columns_body(own, to_near, to_far, rows_near, rows_far):
+    begin, end = (own[:, :128], own[:, WIDTH - 128 :])
+    first = jnp.where(low_lanes(), begin[:64], pltpu.roll(begin[64:], 64, 1))
+    last = jnp.where(low_lanes(), pltpu.roll(end[:64], 64, 1), end[64:])
+    to_near[...], to_far[...] = sides("gz", first, last)
+    rows_near[...], rows_far[...] = sides("xy", own[:RADIUS], own[HEIGHT - RADIUS :])
+
+
+def edges_body(near, far, rows_near, rows_far, halo, to_near, to_far):
+    before, after = sides("gz", near[...], far[...])
+    halo[:64] = jnp.where(low_lanes(), after, pltpu.roll(before, 64, 1))
+    halo[64:] = jnp.where(low_lanes(), pltpu.roll(after, 64, 1), before)
+    first, last = (slice(0, RADIUS), slice(HEIGHT - RADIUS, HEIGHT))
+    to_near[:, :WIDTH] = rows_near[...]
+    to_far[:, :WIDTH] = rows_far[...]
+    to_near[:, WIDTH:], to_far[:, WIDTH:] = sides("xy", halo[first, :], halo[last, :])
+
+
+def forward_body(near, own, halo, far, slopes, pooled, natural):
     before, after = sides("xy", near[...], far[...])
-    padded = jnp.concatenate([before, own[...], after], axis=0)
+    middle = jnp.concatenate([own[...], halo[...]], axis=1)
+    padded = jnp.concatenate([before, middle, after], axis=0)
     matrix = band(HEIGHT, HEIGHT + 2 * RADIUS)
     total = None
     for part in parts_of(padded, 3):
         term = dot(matrix, part)
         total = term if total is None else total + term
     turned = (total * SCALE).T
-    out[...] = turned
-    to_near[...], to_far[...] = sides("gz", turned[:64], turned[WIDTH - 64 :])
-
-
-def forward_body(near, own, far, expo, pooled, natural):
-    left, right = sides("gz", near[...], far[...])
-    padded = jnp.concatenate([left, own[...], right], axis=0)
+    padded = jnp.concatenate([turned[WIDTH + 64 :], turned[: WIDTH + 64]], axis=0)
     padded = jnp.concatenate(parts_of(padded, 3), axis=1)
     matrix = band(192, 256)
     for block in range(3):
@@ -135,8 +167,7 @@
             natural[: 192 - RADIUS, :] = value[RADIUS:]
         else:
             natural[192 * block - RADIUS : 192 * block - RADIUS + 192, :] = value
-    for q in range(SUB):
-        expo[q] = natural[pl.ds(q, CELLS, stride=SUB), :]
+    expo = [natural[pl.ds(q, CELLS, stride=SUB), :] for q in range(SUB)]
     place = place_lanes()
     stacks = []
     for s in range(SLOPES):
@@ -144,7 +175,9 @@
         mean = jnp.zeros((CELLS, HEIGHT), F32)
         slant = jnp.zeros((CELLS, HEIGHT), F32)
         for q in range(SUB):
-            fill = 1.0 / (1.0 + factor * expo[q])
+            scaled = factor * expo[q]
+            fill = 1.0 / (1.0 + scaled)
+            slopes[s, q] = fill * fill * scaled
             mean = mean + fill
             slant = slant + (q - 3.5) * fill
         stacks += [mean, mean * place, slant]
@@ -154,8 +187,8 @@
     pooled[...] = dot(rows, base) * (1.0 / 64.0)
 
 
-def backward_body(expo, pooled, got, out, turned, to_near, to_far, natural):
-    half = iota((1, 128), 1) < 64
+def backward_body(slopes, pooled, got, out, turned, to_near, to_far, natural):
+    half = low_lanes()
 
     def pair(a, b):
         return jnp.where(half, a, b)
@@ -211,11 +244,9 @@
     for q in range(SUB):
         total = jnp.zeros((CELLS, HEIGHT), F32)
         for s in range(SLOPES):
-            scaled = math.exp(0.64 * (s - 2)) * expo[q]
-            fill = 1.0 / (1.0 + scaled)
-            total = total + (fill * fill * scaled) * (flat[s] + (q - 3.5) * tilt[s])
+            total = total + slopes[s, q] * (flat[s] + (q - 3.5) * tilt[s])
         natural[pl.ds(q, CELLS, stride=SUB), :] = total
-    out[...] = natural[:WIDTH, :].T
+    out[...] = natural[:WIDTH, :]
     matrix = band(192, 256)
     pieces = []
     for block in range(3):
@@ -231,12 +262,31 @@
     to_near[...], to_far[...] = sides("xy", result[:RADIUS], result[HEIGHT - RADIUS :])
 
 
-def last_body(near, own, far, out):
+def emit_body(grad, turned, out, result, partial, middle, sem):
+    matrix = band(HEIGHT, HEIGHT + 2 * RADIUS)[:, RADIUS : RADIUS + HEIGHT]
+    high, low = parts_of(turned[...], 2)
+    total = (dot(matrix, high) + dot(matrix, low)) * SCALE
+    middle[...] = total[RADIUS : HEIGHT - RADIUS]
+    copy = pltpu.make_async_copy(middle, result.at[pl.ds(RADIUS, HEIGHT - 2 * RADIUS)], sem)
+    copy.start()
+    partial[:RADIUS] = total[:RADIUS]
+    partial[RADIUS:] = total[HEIGHT - RADIUS :]
+    out[...] = grad[...].T
+    copy.wait()
+
+
+def last_body(near, partial, far, start, result, ends, sems):
     before, after = sides("xy", near[...], far[...])
-    padded = jnp.concatenate([before, own[...], after], axis=0)
-    matrix = band(HEIGHT, HEIGHT + 2 * RADIUS)
-    high, low = parts_of(padded, 2)
-    out[...] = (dot(matrix, high) + dot(matrix, low)) * SCALE
+    matrix = band(RADIUS, 3 * RADIUS)
+    copies = []
+    for index, (rows, weights) in enumerate([(before, matrix[:, :RADIUS]), (after, matrix[:, 2 * RADIUS :])]):
+        high, low = parts_of(rows, 2)
+        ends[index] = partial[RADIUS * index : RADIUS * (index + 1)] + (dot(weights, high) + dot(weights, low)) * SCALE
+        where = result.at[pl.ds((HEIGHT - RADIUS) * index, RADIUS)]
+        copies.append(pltpu.make_async_copy(ends.at[index], where, sems.at[index]))
+        copies[-1].start()
+    for copy in copies:
+        copy.wait()
 
 
 def swap(near, far, axis):
@@ -250,58 +300,67 @@
     return (near, far)
 
 
-def edges_body(density, near, far, sems):
-    first = jnp.where(odd("xy"), 0, HEIGHT - RADIUS)
-    second = HEIGHT - RADIUS - first
-    copies = [
-        pltpu.make_async_copy(density.at[pl.ds(pl.multiple_of(start, RADIUS), RADIUS)], target, sems.at[index])
-        for index, (start, target) in enumerate([(first, near), (second, far)])
-    ]
-    for copy in copies:
-        copy.start()
-    for copy in copies:
-        copy.wait()
-
-
 def steps(density, cotangent, slope, layer_block, block_eps):
-    near, far = pl.pallas_call(
-        edges_body,
-        name="edges",
-        out_shape=[jax.ShapeDtypeStruct((RADIUS, WIDTH), F32)] * 2,
-        in_specs=[pl.BlockSpec(memory_space=pltpu.HBM)],
-        out_specs=[VMEM] * 2,
-        scratch_shapes=[pltpu.SemaphoreType.DMA((2,))],
-        compiler_params=pltpu.CompilerParams(vmem_limit_bytes=60 * 1024 * 1024),
-        cost_estimate=pl.CostEstimate(flops=10**5, bytes_accessed=10**6, transcendentals=0),
-    )(density)
-    near, far = swap(near, far, "xy")
+    shapes = [(64, 128), (64, 128), (RADIUS, WIDTH), (RADIUS, WIDTH)]
+    near, far, *rows = call(columns_body, shapes, [], 10**5, 10**6, density)
+    near, far = swap(near, far, "gz")
     (send,) = pl.pallas_call(
         pack_body,
         name="pack",
         out_shape=[jax.ShapeDtypeStruct((4, ROWS, 128), F32)],
-        in_specs=[pl.BlockSpec(memory_space=pltpu.HBM)] * 4,
-        out_specs=[VMEM],
+        in_specs=[HBM] * 4,
+        out_specs=[HBM],
         scratch_shapes=[
             pltpu.SMEM((4,), jnp.int32),
             pltpu.SMEM((4,), jnp.int32),
             pltpu.SMEM((2, 4), F32),
             pltpu.VMEM((384, 256), F32),
-            pltpu.SemaphoreType.DMA((6,)),
+            pltpu.VMEM((4, ROWS, 128), F32),
+            pltpu.SemaphoreType.DMA((9,)),
         ],
         compiler_params=pltpu.CompilerParams(vmem_limit_bytes=60 * 1024 * 1024),
         cost_estimate=pl.CostEstimate(flops=10**6, bytes_accessed=10**6, transcendentals=0),
     )(slope, layer_block, block_eps.T, cotangent.reshape(384, 256))
     got = lax.all_to_all(send, "gz", 0, 0, tiled=True)
-    across, near, far = (
-        *call(rows_body, [(WIDTH, HEIGHT), (64, HEIGHT), (64, HEIGHT)], [], 10**8, 10**6, near, density, far),
+    edges = [(HEIGHT, 128), (RADIUS, WIDTH + 128), (RADIUS, WIDTH + 128)]
+    halo, near, far = call(edges_body, edges, [], 10**5, 10**6, near, far, *rows)
+    near, far = swap(near, far, "xy")
+    slopes, pooled = call(
+        forward_body,
+        [(SLOPES, SUB, CELLS, HEIGHT), (1088, 256)],
+        [(WIDE, HEIGHT)],
+        10**8,
+        2 * 10**6,
+        near,
+        density,
+        halo,
+        far,
     )
-    near, far = swap(near, far, "gz")
-    expo, pooled = call(forward_body, [(SUB, CELLS, HEIGHT), (1088, 256)], [(WIDE, HEIGHT)], 10**8, 2 * 10**6, near, across, far)
-    own, turned, near, far = call(
-        backward_body, [(HEIGHT, WIDTH), (HEIGHT, WIDTH), (RADIUS, WIDTH), (RADIUS, WIDTH)], [(WIDE, HEIGHT)], 10**8, 3 * 10**6, expo, pooled, got
-    )
+    shapes = [(WIDTH, HEIGHT), (HEIGHT, WIDTH), (RADIUS, WIDTH), (RADIUS, WIDTH)]
+    grad, turned, near, far = call(backward_body, shapes, [(WIDE, HEIGHT)], 10**8, 3 * 10**6, slopes, pooled, got)
     near, far = swap(near, far, "xy")
-    (result,) = call(last_body, [(HEIGHT, WIDTH)], [], 10**8, 10**6, near, turned, far)
+    whole = jax.ShapeDtypeStruct((HEIGHT, WIDTH), F32)
+    own, result, partial = pl.pallas_call(
+        emit_body,
+        name="emit",
+        out_shape=[whole, whole, jax.ShapeDtypeStruct((2 * RADIUS, WIDTH), F32)],
+        in_specs=[VMEM] * 2,
+        out_specs=[VMEM, HBM, VMEM],
+        scratch_shapes=[pltpu.VMEM((HEIGHT - 2 * RADIUS, WIDTH), F32), pltpu.SemaphoreType.DMA],
+        compiler_params=pltpu.CompilerParams(vmem_limit_bytes=LIMIT),
+        cost_estimate=pl.CostEstimate(flops=10**8, bytes_accessed=10**6, transcendentals=0),
+    )(grad, turned)
+    result = pl.pallas_call(
+        last_body,
+        name="last",
+        out_shape=whole,
+        in_specs=[VMEM] * 3 + [HBM],
+        out_specs=HBM,
+        scratch_shapes=[pltpu.VMEM((2, RADIUS, WIDTH), F32), pltpu.SemaphoreType.DMA((2,))],
+        input_output_aliases={3: 0},
+        compiler_params=pltpu.CompilerParams(vmem_limit_bytes=LIMIT),
+        cost_estimate=pl.CostEstimate(flops=10**7, bytes_accessed=10**6, transcendentals=0),
+    )(near, partial, far, result)
     return (own, result)
 
 

time: 58.2 us -> 58.1 us (level)
  the two profiles are of different devices: /device:TPU:22 before, /device:TPU:14 now
where the time goes in v3:
time: 58.1 us; the launch traced here: 57.8 us
  starting transfers between devices  41.9 us (72%)
  waiting for transfers between devices  7.86 us (14%)
  Pallas kernels  7.24 us (12%)
  between operations  0.75 us (1%)
    ppermute x3, starting transfers between devices, swap(): far = lax.ppermute(far, axis, pairs(1))  30.8 us
    ppermute x3, waiting for transfers between devices, swap(): far = lax.ppermute(far, axis, pairs(1))  5.97 us
    ppermute x3, starting transfers between devices, swap(): near = lax.ppermute(near, axis, pairs(0))  5.76 us
    all_to_all x1, starting transfers between devices, steps(): got = lax.all_to_all(send, 'gz', 0, 0, tiled=True)  5.33 us
    pallas_call x4, Pallas kernels, call(): pl.pallas_call(body, out_shape=[jax.ShapeDtypeStruct(shape, F32) for shap...  2.69 us
    pallas_call x1, Pallas kernels, steps(): pl.pallas_call(pack_body, name='pack', out_shape=[jax.ShapeDtypeStruct((4...  2.05 us
    ppermute x3, waiting for transfers between devices, swap(): near = lax.ppermute(near, axis, pairs(0))  1.89 us
    pallas_call x1, Pallas kernels, steps(): pl.pallas_call(emit_body, name='emit', out_shape=[whole, whole, jax.Shape...  1.64 us
  transfers between devices with their start and end apart: 7, of which 4 were waited for; matrix products, arithmetic and copies ran while one was open for 0% of the time, Pallas kernels for 6%

profile of v3, /device:TPU:14, one launch (start us, length us, event | category | flops | bytes accessed | tf_op | source)
XLA Modules:
  0.0 57.8 jit_solution(4010761644522091508)
XLA Ops:
  0.6 0.0 copy-start
  0.6 2.1 %pack.1 = f32[4,224,128]{2,1,0:T(8,128)} custom-call(s32[4]{0:T(128)} %slope_hbm.1, s32[4]{0:T(128)} %block_hbm.1, f32[2,4]{1,0:T(2,128)} %bitcast.3, f32[384,256]{1,0:T(8,128)} %bitcast.2), custom_call_target="tpu_custom_call" | custom-call | flops 1000000 | bytes 1000000 | tf_op jit(solution)/shard_map/pack/pallas_call | solution.py:307
  2.7 5.3 %all-to-all-start = ((f32[4,224,128]{2,1,0:T(8,128)}), f32[4,224,128]{2,1,0:T(8,128)S(1)}, u32[]{:S(2)}, u32[]{:S(2)}) async-start(f32[4,224,128]{2,1,0:T(8,128)} %pack.1), calls=%async_computation | async-start | bytes 917504 | tf_op jit(solution)/shard_map/all_to_all | solution.py:324
  8.0 0.0 copy-done
  8.0 0.1 shard_map.68
  8.1 1.9 %collective-permute-start = (f32[64,128]{1,0:T(8,128)S(1)}, f32[64,128]{1,0:T(8,128)S(1)}, u32[]{:S(2)}, u32[]{:S(2)}) collective-permute-start(f32[64,128]{1,0:T(8,128)S(1)} %get-tuple-element.18), channel_id=1, source_target_pairs={{0,1},{1,0},{2,3},{3,2},{4,5},{5,4},{6,7},{7,6},{8,9},{9,8},{10,11... | collective-permute-start | bytes 98312 | tf_op jit(solution)/shard_map/ppermute | solution.py:299
  10.0 4.8 %collective-permute-start.1 = (f32[64,128]{1,0:T(8,128)S(1)}, f32[64,128]{1,0:T(8,128)S(1)}, u32[]{:S(2)}, u32[]{:S(2)}) collective-permute-start(f32[64,128]{1,0:T(8,128)S(1)} %get-tuple-element.19), channel_id=1, source_target_pairs={{1,2},{2,1},{5,6},{6,5},{9,10},{10,9},{13,14},{14,13},{17,18},{18,... | collective-permute-start | bytes 98312 | tf_op jit(solution)/shard_map/ppermute | solution.py:298
  14.9 1.9 %collective-permute-done.near = f32[64,128]{1,0:T(8,128)S(1)} collective-permute-done((f32[64,128]{1,0:T(8,128)S(1)}, f32[64,128]{1,0:T(8,128)S(1)}, u32[]{:S(2)}, u32[]{:S(2)}) %collective-permute-start) | collective-permute-done | bytes 32800 | tf_op jit(solution)/shard_map/ppermute | solution.py:299
  16.8 3.6 %collective-permute-done.1.far = f32[64,128]{1,0:T(8,128)S(1)} collective-permute-done((f32[64,128]{1,0:T(8,128)S(1)}, f32[64,128]{1,0:T(8,128)S(1)}, u32[]{:S(2)}, u32[]{:S(2)}) %collective-permute-start.1) | collective-permute-done | bytes 32800 | tf_op jit(solution)/shard_map/ppermute | solution.py:298
  20.4 0.1 shard_map.69
  20.5 1.9 %collective-permute-start.2 = (f32[32,640]{1,0:T(8,128)S(1)}, f32[32,640]{1,0:T(8,128)S(1)}, u32[]{:S(2)}, u32[]{:S(2)}) collective-permute-start(f32[32,640]{1,0:T(8,128)S(1)} %get-tuple-element.22), channel_id=1, source_target_pairs={{0,4},{4,0},{8,12},{12,8},{16,20},{20,16},{24,28},{28,24},{32,36},... | collective-permute-start | bytes 245768 | tf_op jit(solution)/shard_map/ppermute | solution.py:299
  22.4 15.4 %collective-permute-start.3 = (f32[32,640]{1,0:T(8,128)S(1)}, f32[32,640]{1,0:T(8,128)S(1)}, u32[]{:S(2)}, u32[]{:S(2)}) collective-permute-start(f32[32,640]{1,0:T(8,128)S(1)} %get-tuple-element.24), channel_id=1, source_target_pairs={{4,8},{8,4},{12,16},{16,12},{20,24},{24,20},{28,32},{32,28},{36,40... | collective-permute-start | bytes 245768 | tf_op jit(solution)/shard_map/ppermute | solution.py:298
  37.8 0.0 collective-permute-done.2.near
  37.8 2.1 %collective-permute-done.3.far = f32[32,640]{1,0:T(8,128)S(1)} collective-permute-done((f32[32,640]{1,0:T(8,128)S(1)}, f32[32,640]{1,0:T(8,128)S(1)}, u32[]{:S(2)}, u32[]{:S(2)}) %collective-permute-start.3) | collective-permute-done | bytes 81952 | tf_op jit(solution)/shard_map/ppermute | solution.py:298
  39.9 1.4 %shard_map.70 = (f32[5,8,72,128]{3,2,1,0:T(8,128)S(1)}, f32[1088,256]{1,0:T(8,128)S(1)}) custom-call(f32[32,640]{1,0:T(8,128)S(1)} %collective-permute-done.2.near, f32[128,512]{1,0:T(8,128)S(1)} %copy-done, f32[128,128]{1,0:T(8,128)S(1)} %get-tuple-element.23.halo, f32[32,640]{1,0:T(8,128)S(1)} %collective-permute-done.3.far), custom_call_target="tpu_custom_call" | custom-call | flops 100000000 | bytes 2000000 | tf_op jit(solution)/shard_map/pallas_call | solution.py:56
  41.3 0.0 all-to-all-done.got
  41.3 1.1 %shard_map.71 = (f32[512,128]{1,0:T(8,128)S(1)}, f32[128,512]{1,0:T(8,128)S(1)}, f32[32,512]{1,0:T(8,128)S(1)}, f32[32,512]{1,0:T(8,128)S(1)}) custom-call(f32[5,8,72,128]{3,2,1,0:T(8,128)S(1)} %get-tuple-element.25.slopes, f32[1088,256]{1,0:T(8,128)S(1)} %get-tuple-element.26.pooled, f32[4,224,128]{2,1,0:T(8,128)S(1)} %all-to-all-done.got), custom_call_target="tpu_custom_call" | custom-call | flops 100000000 | bytes 3000000 | tf_op jit(solution)/shard_map/pallas_call | solution.py:56
  42.5 1.9 %collective-permute-start.4 = (f32[32,512]{1,0:T(8,128)S(1)}, f32[32,512]{1,0:T(8,128)S(1)}, u32[]{:S(2)}, u32[]{:S(2)}) collective-permute-start(f32[32,512]{1,0:T(8,128)S(1)} %get-tuple-element.30), channel_id=1, source_target_pairs={{0,4},{4,0},{8,12},{12,8},{16,20},{20,16},{24,28},{28,24},{32,36},... | collective-permute-start | bytes 196616 | tf_op jit(solution)/shard_map/ppermute | solution.py:299
  44.4 10.6 %collective-permute-start.5 = (f32[32,512]{1,0:T(8,128)S(1)}, f32[32,512]{1,0:T(8,128)S(1)}, u32[]{:S(2)}, u32[]{:S(2)}) collective-permute-start(f32[32,512]{1,0:T(8,128)S(1)} %get-tuple-element.32), channel_id=1, source_target_pairs={{4,8},{8,4},{12,16},{16,12},{20,24},{24,20},{28,32},{32,28},{36,40... | collective-permute-start | bytes 196616 | tf_op jit(solution)/shard_map/ppermute | solution.py:298
  55.0 1.6 %emit.1 = (f32[128,512]{1,0:T(8,128)}, f32[128,512]{1,0:T(8,128)}, f32[64,512]{1,0:T(8,128)S(1)}) custom-call(f32[512,128]{1,0:T(8,128)S(1)} %get-tuple-element.27.grad, f32[128,512]{1,0:T(8,128)S(1)} %get-tuple-element.28.turned), custom_call_target="tpu_custom_call" | custom-call | flops 100000000 | bytes 1000000 | tf_op jit(solution)/shard_map/emit/pallas_call | solution.py:343
  56.6 0.0 collective-permute-done.4.near
  56.6 0.3 collective-permute-done.5.far
  56.9 0.9 %last.1 = f32[128,512]{1,0:T(8,128)} custom-call(f32[32,512]{1,0:T(8,128)S(1)} %collective-permute-done.4.near, f32[64,512]{1,0:T(8,128)S(1)} %get-tuple-element.31.partial, f32[32,512]{1,0:T(8,128)S(1)} %collective-permute-done.5.far, f32[128,512]{1,0:T(8,128)} %get-tuple-element.33.start), custom_call_target="tpu_custom_call", output_to_operand_aliasing={{}: (3, {})} | custom-call | flops 10000000 | bytes 1000000 | tf_op jit(solution)/shard_map/last/pallas_call | solution.py:353
Async XLA Ops:
  0.6 7.4 %copy-start = (f32[128,512]{1,0:T(8,128)S(1)}, f32[128,512]{1,0:T(8,128)}, u32[]{:S(2)}) copy-start(f32[128,512]{1,0:T(8,128)} %own.3) | copy-start | bytes 786436
  2.7 38.6 %all-to-all-start = ((f32[4,224,128]{2,1,0:T(8,128)}), f32[4,224,128]{2,1,0:T(8,128)S(1)}, u32[]{:S(2)}, u32[]{:S(2)}) async-start(f32[4,224,128]{2,1,0:T(8,128)} %pack.1), calls=%async_computation | async-start | bytes 917504 | tf_op jit(solution)/shard_map/all_to_all | solution.py:324
  8.1 8.6 %collective-permute-start = (f32[64,128]{1,0:T(8,128)S(1)}, f32[64,128]{1,0:T(8,128)S(1)}, u32[]{:S(2)}, u32[]{:S(2)}) collective-permute-start(f32[64,128]{1,0:T(8,128)S(1)} %get-tuple-element.18), channel_id=1, source_target_pairs={{0,1},{1,0},{2,3},{3,2},{4,5},{5,4},{6,7},{7,6},{8,9},{9,8},{10,11... | collective-permute-start | bytes 98312 | tf_op jit(solution)/shard_map/ppermute | solution.py:299
  10.0 10.3 %collective-permute-start.1 = (f32[64,128]{1,0:T(8,128)S(1)}, f32[64,128]{1,0:T(8,128)S(1)}, u32[]{:S(2)}, u32[]{:S(2)}) collective-permute-start(f32[64,128]{1,0:T(8,128)S(1)} %get-tuple-element.19), channel_id=1, source_target_pairs={{1,2},{2,1},{5,6},{6,5},{9,10},{10,9},{13,14},{14,13},{17,18},{18,... | collective-permute-start | bytes 98312 | tf_op jit(solution)/shard_map/ppermute | solution.py:298
  20.5 17.4 %collective-permute-start.2 = (f32[32,640]{1,0:T(8,128)S(1)}, f32[32,640]{1,0:T(8,128)S(1)}, u32[]{:S(2)}, u32[]{:S(2)}) collective-permute-start(f32[32,640]{1,0:T(8,128)S(1)} %get-tuple-element.22), channel_id=1, source_target_pairs={{0,4},{4,0},{8,12},{12,8},{16,20},{20,16},{24,28},{28,24},{32,36},... | collective-permute-start | bytes 245768 | tf_op jit(solution)/shard_map/ppermute | solution.py:299
  22.4 17.5 %collective-permute-start.3 = (f32[32,640]{1,0:T(8,128)S(1)}, f32[32,640]{1,0:T(8,128)S(1)}, u32[]{:S(2)}, u32[]{:S(2)}) collective-permute-start(f32[32,640]{1,0:T(8,128)S(1)} %get-tuple-element.24), channel_id=1, source_target_pairs={{4,8},{8,4},{12,16},{16,12},{20,24},{24,20},{28,32},{32,28},{36,40... | collective-permute-start | bytes 245768 | tf_op jit(solution)/shard_map/ppermute | solution.py:298
  42.5 14.1 %collective-permute-start.4 = (f32[32,512]{1,0:T(8,128)S(1)}, f32[32,512]{1,0:T(8,128)S(1)}, u32[]{:S(2)}, u32[]{:S(2)}) collective-permute-start(f32[32,512]{1,0:T(8,128)S(1)} %get-tuple-element.30), channel_id=1, source_target_pairs={{0,4},{4,0},{8,12},{12,8},{16,20},{20,16},{24,28},{28,24},{32,36},... | collective-permute-start | bytes 196616 | tf_op jit(solution)/shard_map/ppermute | solution.py:299
  44.4 12.5 %collective-permute-start.5 = (f32[32,512]{1,0:T(8,128)S(1)}, f32[32,512]{1,0:T(8,128)S(1)}, u32[]{:S(2)}, u32[]{:S(2)}) collective-permute-start(f32[32,512]{1,0:T(8,128)S(1)} %get-tuple-element.32), channel_id=1, source_target_pairs={{4,8},{8,4},{12,16},{16,12},{20,24},{24,20},{28,32},{32,28},{36,40... | collective-permute-start | bytes 196616 | tf_op jit(solution)/shard_map/ppermute | solution.py:298

commit v4 on v3

--- a/solution.py
+++ b/solution.py
@@ -145,8 +145,8 @@
     to_near[:, WIDTH:], to_far[:, WIDTH:] = sides("xy", halo[first, :], halo[last, :])
 
 
-def forward_body(near, own, halo, far, slopes, pooled, natural):
-    before, after = sides("xy", near[...], far[...])
+def forward_body(own, halo, near, down, up, slopes, pooled, natural):
+    before, after = sides("xy", near[...], jnp.where(odd("xy"), up[...], down[...]))
     middle = jnp.concatenate([own[...], halo[...]], axis=1)
     padded = jnp.concatenate([before, middle, after], axis=0)
     matrix = band(HEIGHT, HEIGHT + 2 * RADIUS)
@@ -262,20 +262,23 @@
     to_near[...], to_far[...] = sides("xy", result[:RADIUS], result[HEIGHT - RADIUS :])
 
 
-def emit_body(grad, turned, out, result, partial, middle, sem):
+def emit_body(grad, turned, out, result, partial, whole, middle, sems):
+    whole[...] = grad[...].T
+    copies = [pltpu.make_async_copy(whole, out, sems.at[0])]
+    copies[0].start()
     matrix = band(HEIGHT, HEIGHT + 2 * RADIUS)[:, RADIUS : RADIUS + HEIGHT]
     high, low = parts_of(turned[...], 2)
     total = (dot(matrix, high) + dot(matrix, low)) * SCALE
     middle[...] = total[RADIUS : HEIGHT - RADIUS]
-    copy = pltpu.make_async_copy(middle, result.at[pl.ds(RADIUS, HEIGHT - 2 * RADIUS)], sem)
-    copy.start()
+    copies.append(pltpu.make_async_copy(middle, result.at[pl.ds(RADIUS, HEIGHT - 2 * RADIUS)], sems.at[1]))
+    copies[1].start()
     partial[:RADIUS] = total[:RADIUS]
     partial[RADIUS:] = total[HEIGHT - RADIUS :]
-    out[...] = grad[...].T
-    copy.wait()
-
-
-def last_body(near, partial, far, start, result, ends, sems):
+    for copy in copies:
+        copy.wait()
+
+
+def last_body(near, far, partial, start, result, ends, sems):
     before, after = sides("xy", near[...], far[...])
     matrix = band(RADIUS, 3 * RADIUS)
     copies = []
@@ -289,15 +292,18 @@
         copy.wait()
 
 
+def pairs(axis, start):
+    return [(i, i + 1) for i in range(start, lax.axis_size(axis) - 1, 2)]
+
+
+def back(steps):
+    return [(j, i) for i, j in steps]
+
+
 def swap(near, far, axis):
-    count = lax.axis_size(axis)
-
-    def pairs(start):
-        return [p for i in range(start, count - 1, 2) for p in ((i, i + 1), (i + 1, i))]
-
-    far = lax.ppermute(far, axis, pairs(1))
-    near = lax.ppermute(near, axis, pairs(0))
-    return (near, far)
+    inner, outer = (pairs(axis, 0), pairs(axis, 1))
+    far = lax.ppermute(far, axis, outer + back(outer))
+    return (lax.ppermute(near, axis, inner + back(inner)), far)
 
 
 def steps(density, cotangent, slope, layer_block, block_eps):
@@ -324,17 +330,21 @@
     got = lax.all_to_all(send, "gz", 0, 0, tiled=True)
     edges = [(HEIGHT, 128), (RADIUS, WIDTH + 128), (RADIUS, WIDTH + 128)]
     halo, near, far = call(edges_body, edges, [], 10**5, 10**6, near, far, *rows)
-    near, far = swap(near, far, "xy")
+    inner, outer = (pairs("xy", 0), pairs("xy", 1))
+    down = lax.ppermute(far, "xy", outer)
+    up = lax.ppermute(far, "xy", back(outer))
+    near = lax.ppermute(near, "xy", inner + back(inner))
     slopes, pooled = call(
         forward_body,
         [(SLOPES, SUB, CELLS, HEIGHT), (1088, 256)],
         [(WIDE, HEIGHT)],
         10**8,
         2 * 10**6,
-        near,
         density,
         halo,
-        far,
+        near,
+        down,
+        up,
     )
     shapes = [(WIDTH, HEIGHT), (HEIGHT, WIDTH), (RADIUS, WIDTH), (RADIUS, WIDTH)]
     grad, turned, near, far = call(backward_body, shapes, [(WIDE, HEIGHT)], 10**8, 3 * 10**6, slopes, pooled, got)
@@ -345,8 +355,12 @@
         name="emit",
         out_shape=[whole, whole, jax.ShapeDtypeStruct((2 * RADIUS, WIDTH), F32)],
         in_specs=[VMEM] * 2,
-        out_specs=[VMEM, HBM, VMEM],
-        scratch_shapes=[pltpu.VMEM((HEIGHT - 2 * RADIUS, WIDTH), F32), pltpu.SemaphoreType.DMA],
+        out_specs=[HBM, HBM, VMEM],
+        scratch_shapes=[
+            pltpu.VMEM((HEIGHT, WIDTH), F32),
+            pltpu.VMEM((HEIGHT - 2 * RADIUS, WIDTH), F32),
+            pltpu.SemaphoreType.DMA((2,)),
+        ],
         compiler_params=pltpu.CompilerParams(vmem_limit_bytes=LIMIT),
         cost_estimate=pl.CostEstimate(flops=10**8, bytes_accessed=10**6, transcendentals=0),
     )(grad, turned)
@@ -360,7 +374,7 @@
         input_output_aliases={3: 0},
         compiler_params=pltpu.CompilerParams(vmem_limit_bytes=LIMIT),
         cost_estimate=pl.CostEstimate(flops=10**7, bytes_accessed=10**6, transcendentals=0),
-    )(near, partial, far, result)
+    )(near, far, partial, result)
     return (own, result)
 
 

time: 58.1 us -> 68.7 us (1.18)
  waiting for transfers between devices: 7.86 us -> 26.4 us
  starting transfers between devices: 41.9 us -> 34.5 us
    ppermute x6 -> x7, waiting for transfers between devices: 7.86 us -> 26.4 us  [the longest x2 13.2 us: swap(): far = lax.ppermute(far, axis, outer + back(outer))]
    ppermute x6 -> x7, starting transfers between devices: 36.6 us -> 29.2 us  [the longest x1 15.4 us: steps(): up = lax.ppermute(far, 'xy', back(outer))]
  transfers between devices with their start and end apart: 7 -> 8, of which waited for: 4 -> 5; matrix products, arithmetic and copies ran while one was open for 0% -> 0% of each run, Pallas kernels for 6% -> 4%
where the time goes in v4:
time: 68.7 us; the launch traced here: 68.3 us
  starting transfers between devices  34.5 us (50%)
  waiting for transfers between devices  26.4 us (38%)
  Pallas kernels  6.6 us (10%)
  between operations  0.76 us (1%)
    ppermute x1, starting transfers between devices, steps(): up = lax.ppermute(far, 'xy', back(outer))  15.4 us
    ppermute x2, waiting for transfers between devices, swap(): far = lax.ppermute(far, axis, outer + back(outer))  13.2 us
    ppermute x1, waiting for transfers between devices, steps(): down = lax.ppermute(far, 'xy', outer)  10.6 us
    ppermute x2, starting transfers between devices, swap(): far = lax.ppermute(far, axis, outer + back(outer))  6.74 us
    all_to_all x1, starting transfers between devices, steps(): got = lax.all_to_all(send, 'gz', 0, 0, tiled=True)  5.33 us
    ppermute x2, starting transfers between devices, swap(): return (lax.ppermute(near, axis, inner + back(inner)), far)  3.84 us
    pallas_call x4, Pallas kernels, call(): pl.pallas_call(body, out_shape=[jax.ShapeDtypeStruct(shape, F32) for shap...  2.69 us
    pallas_call x1, Pallas kernels, steps(): pl.pallas_call(pack_body, name='pack', out_shape=[jax.ShapeDtypeStruct((4...  2.06 us
  transfers between devices with their start and end apart: 8, of which 5 were waited for; matrix products, arithmetic and copies ran while one was open for 0% of the time, Pallas kernels for 4%

profile of v4, /device:TPU:14, one launch (start us, length us, event | category | flops | bytes accessed | tf_op | source)
XLA Modules:
  0.0 68.3 jit_solution(10434623771862363462)
XLA Ops:
  0.6 0.0 copy-start
  0.6 2.1 %pack.1 = f32[4,224,128]{2,1,0:T(8,128)} custom-call(s32[4]{0:T(128)} %slope_hbm.1, s32[4]{0:T(128)} %block_hbm.1, f32[2,4]{1,0:T(2,128)} %bitcast.3, f32[384,256]{1,0:T(8,128)} %bitcast.2), custom_call_target="tpu_custom_call" | custom-call | flops 1000000 | bytes 1000000 | tf_op jit(solution)/shard_map/pack/pallas_call | solution.py:313
  2.7 5.3 %all-to-all-start = ((f32[4,224,128]{2,1,0:T(8,128)}), f32[4,224,128]{2,1,0:T(8,128)S(1)}, u32[]{:S(2)}, u32[]{:S(2)}) async-start(f32[4,224,128]{2,1,0:T(8,128)} %pack.1), calls=%async_computation | async-start | bytes 917504 | tf_op jit(solution)/shard_map/all_to_all | solution.py:330
  8.0 0.1 shard_map.68
  8.1 1.9 %collective-permute-start = (f32[64,128]{1,0:T(8,128)S(1)}, f32[64,128]{1,0:T(8,128)S(1)}, u32[]{:S(2)}, u32[]{:S(2)}) collective-permute-start(f32[64,128]{1,0:T(8,128)S(1)} %get-tuple-element.18), channel_id=1, source_target_pairs={{0,1},{2,3},{1,0},{3,2},{4,5},{6,7},{5,4},{7,6},{8,9},{10,11},{9,8... | collective-permute-start | bytes 98312 | tf_op jit(solution)/shard_map/ppermute | solution.py:306
  10.1 4.8 %collective-permute-start.1 = (f32[64,128]{1,0:T(8,128)S(1)}, f32[64,128]{1,0:T(8,128)S(1)}, u32[]{:S(2)}, u32[]{:S(2)}) collective-permute-start(f32[64,128]{1,0:T(8,128)S(1)} %get-tuple-element.19), channel_id=1, source_target_pairs={{1,2},{2,1},{5,6},{6,5},{9,10},{10,9},{13,14},{14,13},{17,18},{18,... | collective-permute-start | bytes 98312 | tf_op jit(solution)/shard_map/ppermute | solution.py:305
  14.9 1.9 %collective-permute-done.near = f32[64,128]{1,0:T(8,128)S(1)} collective-permute-done((f32[64,128]{1,0:T(8,128)S(1)}, f32[64,128]{1,0:T(8,128)S(1)}, u32[]{:S(2)}, u32[]{:S(2)}) %collective-permute-start) | collective-permute-done | bytes 32800 | tf_op jit(solution)/shard_map/ppermute | solution.py:306
  16.8 3.6 %collective-permute-done.1.far = f32[64,128]{1,0:T(8,128)S(1)} collective-permute-done((f32[64,128]{1,0:T(8,128)S(1)}, f32[64,128]{1,0:T(8,128)S(1)}, u32[]{:S(2)}, u32[]{:S(2)}) %collective-permute-start.1) | collective-permute-done | bytes 32800 | tf_op jit(solution)/shard_map/ppermute | solution.py:305
  20.4 0.1 shard_map.69
  20.5 1.9 %collective-permute-start.2 = (f32[32,640]{1,0:T(8,128)S(1)}, f32[32,640]{1,0:T(8,128)S(1)}, u32[]{:S(2)}, u32[]{:S(2)}) collective-permute-start(f32[32,640]{1,0:T(8,128)S(1)} %get-tuple-element.23), channel_id=1, source_target_pairs={{0,4},{8,12},{16,20},{24,28},{32,36},{40,44},{48,52},{56,60},{64,6... | collective-permute-start | bytes 245768 | tf_op jit(solution)/shard_map/ppermute | solution.py:336
  22.4 15.4 %collective-permute-start.4 = (f32[32,640]{1,0:T(8,128)S(1)}, f32[32,640]{1,0:T(8,128)S(1)}, u32[]{:S(2)}, u32[]{:S(2)}) collective-permute-start(f32[32,640]{1,0:T(8,128)S(1)} %get-tuple-element.24), channel_id=1, source_target_pairs={{8,4},{16,12},{24,20},{32,28},{40,36},{48,44},{56,52},{64,60},{72,... | collective-permute-start | bytes 245768 | tf_op jit(solution)/shard_map/ppermute | solution.py:335
  37.8 1.3 %collective-permute-start.3 = (f32[32,640]{1,0:T(8,128)S(1)}, f32[32,640]{1,0:T(8,128)S(1)}, u32[]{:S(2)}, u32[]{:S(2)}) collective-permute-start(f32[32,640]{1,0:T(8,128)S(1)} %get-tuple-element.24), channel_id=1, source_target_pairs={{4,8},{12,16},{20,24},{28,32},{36,40},{44,48},{52,56},{60,64},{68,... | collective-permute-start | bytes 245768 | tf_op jit(solution)/shard_map/ppermute | solution.py:334
  39.1 0.0 collective-permute-done.2.near
  39.1 0.7 %collective-permute-done.4.up = f32[32,640]{1,0:T(8,128)S(1)} collective-permute-done((f32[32,640]{1,0:T(8,128)S(1)}, f32[32,640]{1,0:T(8,128)S(1)}, u32[]{:S(2)}, u32[]{:S(2)}) %collective-permute-start.4) | collective-permute-done | bytes 81952 | tf_op jit(solution)/shard_map/ppermute | solution.py:335
  39.9 10.6 %collective-permute-done.3.down = f32[32,640]{1,0:T(8,128)S(1)} collective-permute-done((f32[32,640]{1,0:T(8,128)S(1)}, f32[32,640]{1,0:T(8,128)S(1)}, u32[]{:S(2)}, u32[]{:S(2)}) %collective-permute-start.3) | collective-permute-done | bytes 81952 | tf_op jit(solution)/shard_map/ppermute | solution.py:334
  50.5 1.4 %shard_map.70 = (f32[5,8,72,128]{3,2,1,0:T(8,128)S(1)}, f32[1088,256]{1,0:T(8,128)S(1)}) custom-call(f32[128,512]{1,0:T(8,128)S(1)} %copy-done, f32[128,128]{1,0:T(8,128)S(1)} %get-tuple-element.22.halo, f32[32,640]{1,0:T(8,128)S(1)} %collective-permute-done.2.near, f32[32,640]{1,0:T(8,128)S(1)} %collective-permute-done.3.down, ...), custom_call_target="tpu_custom_call" | custom-call | flops 100000000 | bytes 2000000 | tf_op jit(solution)/shard_map/pallas_call | solution.py:56
  51.9 0.0 all-to-all-done.got
  51.9 1.1 %shard_map.71 = (f32[512,128]{1,0:T(8,128)S(1)}, f32[128,512]{1,0:T(8,128)S(1)}, f32[32,512]{1,0:T(8,128)S(1)}, f32[32,512]{1,0:T(8,128)S(1)}) custom-call(f32[5,8,72,128]{3,2,1,0:T(8,128)S(1)} %get-tuple-element.25.slopes, f32[1088,256]{1,0:T(8,128)S(1)} %get-tuple-element.26.pooled, f32[4,224,128]{2,1,0:T(8,128)S(1)} %all-to-all-done.got), custom_call_target="tpu_custom_call" | custom-call | flops 100000000 | bytes 3000000 | tf_op jit(solution)/shard_map/pallas_call | solution.py:56
  53.0 1.9 %collective-permute-start.5 = (f32[32,512]{1,0:T(8,128)S(1)}, f32[32,512]{1,0:T(8,128)S(1)}, u32[]{:S(2)}, u32[]{:S(2)}) collective-permute-start(f32[32,512]{1,0:T(8,128)S(1)} %get-tuple-element.30), channel_id=1, source_target_pairs={{0,4},{8,12},{16,20},{24,28},{32,36},{40,44},{48,52},{56,60},{64,6... | collective-permute-start | bytes 196616 | tf_op jit(solution)/shard_map/ppermute | solution.py:306
  55.0 1.9 %collective-permute-start.6 = (f32[32,512]{1,0:T(8,128)S(1)}, f32[32,512]{1,0:T(8,128)S(1)}, u32[]{:S(2)}, u32[]{:S(2)}) collective-permute-start(f32[32,512]{1,0:T(8,128)S(1)} %get-tuple-element.31), channel_id=1, source_target_pairs={{4,8},{12,16},{20,24},{28,32},{36,40},{44,48},{52,56},{60,64},{68,... | collective-permute-start | bytes 196616 | tf_op jit(solution)/shard_map/ppermute | solution.py:305
  56.9 1.0 %emit.1 = (f32[128,512]{1,0:T(8,128)}, f32[128,512]{1,0:T(8,128)}, f32[64,512]{1,0:T(8,128)S(1)}) custom-call(f32[512,128]{1,0:T(8,128)S(1)} %get-tuple-element.27.grad, f32[128,512]{1,0:T(8,128)S(1)} %get-tuple-element.28.turned), custom_call_target="tpu_custom_call" | custom-call | flops 100000000 | bytes 1000000 | tf_op jit(solution)/shard_map/emit/pallas_call | solution.py:353
  57.9 0.0 collective-permute-done.5.near
  57.9 9.6 %collective-permute-done.6.far = f32[32,512]{1,0:T(8,128)S(1)} collective-permute-done((f32[32,512]{1,0:T(8,128)S(1)}, f32[32,512]{1,0:T(8,128)S(1)}, u32[]{:S(2)}, u32[]{:S(2)}) %collective-permute-start.6) | collective-permute-done | bytes 65568 | tf_op jit(solution)/shard_map/ppermute | solution.py:305
  67.5 0.9 %last.1 = f32[128,512]{1,0:T(8,128)} custom-call(f32[32,512]{1,0:T(8,128)S(1)} %collective-permute-done.5.near, f32[32,512]{1,0:T(8,128)S(1)} %collective-permute-done.6.far, f32[64,512]{1,0:T(8,128)S(1)} %get-tuple-element.32.partial, f32[128,512]{1,0:T(8,128)} %get-tuple-element.33.start), custom_call_target="tpu_custom_call", output_to_operand_aliasing={{}: (3, {})} | custom-call | flops 10000000 | bytes 1000000 | tf_op jit(solution)/shard_map/last/pallas_call | solution.py:367
  (1 shorter events, 0.0 us)
Async XLA Ops:
  0.6 7.4 %copy-start = (f32[128,512]{1,0:T(8,128)S(1)}, f32[128,512]{1,0:T(8,128)}, u32[]{:S(2)}) copy-start(f32[128,512]{1,0:T(8,128)} %own.3) | copy-start | bytes 786436
  2.7 49.2 %all-to-all-start = ((f32[4,224,128]{2,1,0:T(8,128)}), f32[4,224,128]{2,1,0:T(8,128)S(1)}, u32[]{:S(2)}, u32[]{:S(2)}) async-start(f32[4,224,128]{2,1,0:T(8,128)} %pack.1), calls=%async_computation | async-start | bytes 917504 | tf_op jit(solution)/shard_map/all_to_all | solution.py:330
  8.1 8.6 %collective-permute-start = (f32[64,128]{1,0:T(8,128)S(1)}, f32[64,128]{1,0:T(8,128)S(1)}, u32[]{:S(2)}, u32[]{:S(2)}) collective-permute-start(f32[64,128]{1,0:T(8,128)S(1)} %get-tuple-element.18), channel_id=1, source_target_pairs={{0,1},{2,3},{1,0},{3,2},{4,5},{6,7},{5,4},{7,6},{8,9},{10,11},{9,8... | collective-permute-start | bytes 98312 | tf_op jit(solution)/shard_map/ppermute | solution.py:306
  10.1 10.3 %collective-permute-start.1 = (f32[64,128]{1,0:T(8,128)S(1)}, f32[64,128]{1,0:T(8,128)S(1)}, u32[]{:S(2)}, u32[]{:S(2)}) collective-permute-start(f32[64,128]{1,0:T(8,128)S(1)} %get-tuple-element.19), channel_id=1, source_target_pairs={{1,2},{2,1},{5,6},{6,5},{9,10},{10,9},{13,14},{14,13},{17,18},{18,... | collective-permute-start | bytes 98312 | tf_op jit(solution)/shard_map/ppermute | solution.py:305
  20.5 18.7 %collective-permute-start.2 = (f32[32,640]{1,0:T(8,128)S(1)}, f32[32,640]{1,0:T(8,128)S(1)}, u32[]{:S(2)}, u32[]{:S(2)}) collective-permute-start(f32[32,640]{1,0:T(8,128)S(1)} %get-tuple-element.23), channel_id=1, source_target_pairs={{0,4},{8,12},{16,20},{24,28},{32,36},{40,44},{48,52},{56,60},{64,6... | collective-permute-start | bytes 245768 | tf_op jit(solution)/shard_map/ppermute | solution.py:336
  22.4 17.5 %collective-permute-start.4 = (f32[32,640]{1,0:T(8,128)S(1)}, f32[32,640]{1,0:T(8,128)S(1)}, u32[]{:S(2)}, u32[]{:S(2)}) collective-permute-start(f32[32,640]{1,0:T(8,128)S(1)} %get-tuple-element.24), channel_id=1, source_target_pairs={{8,4},{16,12},{24,20},{32,28},{40,36},{48,44},{56,52},{64,60},{72,... | collective-permute-start | bytes 245768 | tf_op jit(solution)/shard_map/ppermute | solution.py:335
  37.8 12.7 %collective-permute-start.3 = (f32[32,640]{1,0:T(8,128)S(1)}, f32[32,640]{1,0:T(8,128)S(1)}, u32[]{:S(2)}, u32[]{:S(2)}) collective-permute-start(f32[32,640]{1,0:T(8,128)S(1)} %get-tuple-element.24), channel_id=1, source_target_pairs={{4,8},{12,16},{20,24},{28,32},{36,40},{44,48},{52,56},{60,64},{68,... | collective-permute-start | bytes 245768 | tf_op jit(solution)/shard_map/ppermute | solution.py:334
  53.0 4.9 %collective-permute-start.5 = (f32[32,512]{1,0:T(8,128)S(1)}, f32[32,512]{1,0:T(8,128)S(1)}, u32[]{:S(2)}, u32[]{:S(2)}) collective-permute-start(f32[32,512]{1,0:T(8,128)S(1)} %get-tuple-element.30), channel_id=1, source_target_pairs={{0,4},{8,12},{16,20},{24,28},{32,36},{40,44},{48,52},{56,60},{64,6... | collective-permute-start | bytes 196616 | tf_op jit(solution)/shard_map/ppermute | solution.py:306
  55.0 12.5 %collective-permute-start.6 = (f32[32,512]{1,0:T(8,128)S(1)}, f32[32,512]{1,0:T(8,128)S(1)}, u32[]{:S(2)}, u32[]{:S(2)}) collective-permute-start(f32[32,512]{1,0:T(8,128)S(1)} %get-tuple-element.31), channel_id=1, source_target_pairs={{4,8},{12,16},{20,24},{28,32},{36,40},{44,48},{52,56},{60,64},{68,... | collective-permute-start | bytes 196616 | tf_op jit(solution)/shard_map/ppermute | solution.py:305
